TPU v7x, 32 devices: a whole 2x2x4 slice. The times are simulated.
32 devices in a mesh: lon: 8 (over z, x), lat: 4 (over y, core).
Axes of the slice: x: 2, y: 2, z: 4, core: 2. Of those that a mesh axis runs over, the one named last changes fastest.
Arguments:
- kappa_east: float32 [64, 1024], P('lat', 'lon'), may hold values from 0.02 to 0.2
- kappa_north: float32 [64, 1024], P('lat', 'lon'), may hold values from 0.02 to 0.2
- depth: int32 [64, 1024], P('lat', 'lon'), may hold values from 0 to 75
- sigma: float32 [151], replicated, may hold values from 0.3 to 3
- obs_precision: float32 [151], replicated, may hold values from 0.5 to 4
- obs_tile: int32 [4096, 1], P(('lon', 'lat')), may hold values from 0 to 7; in each aligned block of 128 rows (0 to 127, 128 to 255, ...) at most 32 rows name the same one
- obs_col: int32 [4096], P(('lon', 'lat')), may hold values from 0 to 127
- obs_lat: int32 [4096], P(('lon', 'lat')), may hold values from 0 to 15
- innovation: float32 [151, 4096], P(None, ('lon', 'lat')), may hold values from -6 to 6
Outputs:
- increment: float32 [151, 64, 1024], P(None, 'lat', 'lon')
- residual: float32 [151, 64, 1024], P(None, 'lat', 'lon')
Inputs may be any that keep to these rules, and one draw needn't show every extreme that they name: `obs_tile`: among the 128 profiles listed on one device, no longitude tile is named by more than 32, a bound that some block reaches.
All inputs are finite; a program needn't handle non-finite values.
Results may differ from a plain program's by a relative error of at most 0.00013.
Values sent between devices are 32-bit elements; how exact they have to be, the bound alone decides.
A program may use at most 128 MiB of HBM per device.

v0:
```python
import functools

import jax
import jax.numpy as jnp
from jax import lax
from jax.experimental import pallas as pl
from jax.experimental.pallas import tpu as pltpu
from jax.sharding import PartitionSpec as P

MESH = pl.DeviceIdType.MESH
SUB = 8
PACK = 4
PASSES = 5
STAGES = 5
STRIDE = 32
OWN = 2 * PASSES
EAST = 16


def split3(x):
    high = x.astype(jnp.bfloat16)
    left = x - high.astype(jnp.float32)
    middle = left.astype(jnp.bfloat16)
    low = (left - middle.astype(jnp.float32)).astype(jnp.bfloat16)
    return high, middle, low


def place_of(row, rows):
    starts = [0, PASSES, 2 * PASSES, rows, rows + PASSES]
    a = max(i for i, s in enumerate(starts) if row >= s)
    return a, row - starts[a]


def main_kernel(
    tiles,
    bands,
    cap,
    total,
    data,
    tile_row,
    tile_col,
    maps,
    coef,
    v_out,
    c_out,
    pay,
    rcv,
    parts,
    table,
    near,
    ext,
    strip,
    base,
    f,
    fe,
    fn,
    res,
    gain,
    hs,
    hn,
    pw,
    pe,
    pk,
    mom,
    red,
    red_lat,
    red_lon,
    obs_send,
    obs_recv,
    map_send,
    map_recv,
    own_sem,
    halo_send,
    halo_recv,
    sum_send,
    sum_recv,
):
    lon, lat = lax.axis_index("lon"), lax.axis_index("lat")
    rows, lanes = maps.shape[1], maps.shape[2]
    quads = f.shape[0]
    deep = rows + 2 * PASSES
    last = rows + PASSES
    has_s, has_n = lat > 0, lat < bands - 1

    def at(dl, db):
        return lax.rem(lon + dl + tiles, tiles), lax.rem(lat + db + bands, bands)

    beside = [(lon, lax.rem(lat + k, bands)) for k in range(1, bands)]
    along = [(lax.rem(lon + k, tiles), lat) for k in range(1, tiles)]
    ways = [(0, -1), (0, 1), (-1, 0), (1, 0), (-1, -1), (1, -1), (-1, 1), (1, 1)]
    there = {-1: has_s, 0: None, 1: has_n}

    def only(cond, body):
        if cond is None:
            body()
        else:
            pl.when(cond)(body)

    barrier = pltpu.get_barrier_semaphore()

    def greet(peer):
        pl.semaphore_signal(barrier, inc=1, device_id=peer, device_id_type=MESH)

    for peer in beside + along:
        greet(peer)
    for dl, db in ways[4:]:
        only(there[db], functools.partial(greet, at(dl, db)))

    def remote(src, dst, send, recv, peer):
        return pltpu.make_async_remote_copy(
            src_ref=src,
            dst_ref=dst,
            send_sem=send,
            recv_sem=recv,
            device_id=peer,
            device_id_type=MESH,
        )

    listed = tile_row.shape[1]
    slots = tiles * cap
    same = tile_col[...] == tile_row[...]
    earlier = lax.broadcasted_iota(jnp.int32, (listed, listed), 0) < lax.broadcasted_iota(
        jnp.int32, (listed, listed), 1
    )
    rank = jnp.sum(jnp.where(same & earlier, 1.0, 0.0), 0, keepdims=True)
    slot = tile_row[...] * cap + rank.astype(jnp.int32)
    chosen = lax.broadcasted_iota(jnp.int32, (slots, listed), 0) == slot
    chosen = jnp.where(chosen, 1.0, 0.0).astype(jnp.bfloat16)
    width = data.shape[0]
    packed = jnp.zeros((slots, width), jnp.float32)
    for part in split3(data[...]):
        packed = packed + lax.dot_general(
            chosen, part, (((1,), (1,)), ((), ())), preferred_element_type=jnp.float32
        )
    pay[...] = packed.reshape(tiles, cap, width)

    diagonal = jnp.where(has_s, 2, 0) + jnp.where(has_n, 2, 0)
    pl.semaphore_wait(barrier, len(beside) + len(along) + diagonal)

    def slot_of(dl, db):
        return (dl + 1) * 3 + db + 1

    def map_copy(d):
        dl, db = ways[d]
        return remote(
            maps, near.at[slot_of(-dl, -db)], map_send.at[d], map_recv.at[d], at(dl, db)
        )

    for d in (4, 5, 6, 7, 2, 3, 0, 1):
        only(there[ways[d][1]], lambda d=d: map_copy(d).start())
    obs = []
    for k, peer in enumerate(along):
        copy = remote(pay.at[peer[0]], rcv.at[lon], obs_send.at[k], obs_recv.at[k], peer)
        copy.start()
        obs.append(copy)
    own = pltpu.make_async_copy(pay.at[lon], rcv.at[lon], own_sem)
    own.start()

    zero = jnp.zeros((SUB, lanes), jnp.float32)
    nothing = jnp.zeros(maps.shape, jnp.float32)
    near[slot_of(0, 0)] = maps[...]
    for dl in (-1, 0, 1):

        @pl.when(jnp.logical_not(has_s))
        def _(dl=dl):
            near[slot_of(dl, -1)] = nothing

        @pl.when(jnp.logical_not(has_n))
        def _(dl=dl):
            near[slot_of(dl, 1)] = nothing

    @pl.when(jnp.logical_not(has_s))
    def _():
        hs[...] = jnp.zeros(hs.shape, jnp.float32)
        pw[:, :, 0] = jnp.zeros(pw.shape[:2] + pw.shape[3:], jnp.float32)
        pe[:, :, 0] = jnp.zeros(pe.shape[:2] + pe.shape[3:], jnp.float32)

    @pl.when(jnp.logical_not(has_n))
    def _():
        hn[...] = jnp.zeros(hn.shape, jnp.float32)
        pw[:, :, 4] = jnp.zeros(pw.shape[:2] + pw.shape[3:], jnp.float32)
        pe[:, :, 4] = jnp.zeros(pe.shape[:2] + pe.shape[3:], jnp.float32)

    for i in range(STAGES):
        mom[i] = zero
    red[...] = zero
    ext[...] = jnp.zeros(ext.shape, jnp.float32)
    strip[...] = jnp.zeros(strip.shape, jnp.float32)

    for d in range(8):
        dl, db = ways[d]
        only(there[-db], lambda d=d: map_copy(d).wait_recv())
    for d in range(8):
        only(there[ways[d][1]], lambda d=d: map_copy(d).wait_send())

    for m in range(3):
        for side in range(3):
            ext[m, side, 0:PASSES] = near[3 * side, m, rows - PASSES : rows]
            ext[m, side, PASSES:last] = near[3 * side + 1, m]
            ext[m, side, last:deep] = near[3 * side + 2, m, 0:PASSES]
    padded = -(-deep // SUB) * SUB
    lane = lax.broadcasted_iota(jnp.int32, (padded, lanes), 1)
    part_of, within = lane // STRIDE, lane % STRIDE
    for m in range(3):
        west, mid, east = (ext[m, side, 0:padded] for side in range(3))
        out = jnp.zeros((padded, lanes), jnp.float32)
        for k in range(PACK):
            here, start = part_of == k, STRIDE * k
            pieces = (
                (west, lanes - PASSES, 0, PASSES),
                (mid, 0, PASSES, OWN),
                (mid, lanes - OWN, EAST, OWN),
                (east, 0, EAST + OWN, PASSES),
            )
            for source, column, first, count in pieces:
                moved = pltpu.roll(source, (start + first - column) % lanes, 1)
                inside = here & (within >= first) & (within < first + count)
                out = jnp.where(inside, moved, out)
        strip[m, 0:padded] = out
    for i, (ke, kn, depth, above) in enumerate(
        (
            (ext[0, 1, 0:padded], ext[1, 1, 0:padded], ext[2, 1, 0:padded], ext[2, 1, 1 : padded + 1]),
            (strip[0, 0:padded], strip[1, 0:padded], strip[2, 0:padded], strip[2, 1 : padded + 1]),
        )
    ):
        base[i, 0] = ke
        base[i, 1] = jnp.minimum(depth, pltpu.roll(depth, lanes - 1, 1))
        base[i, 2] = kn
        base[i, 3] = jnp.minimum(depth, above)

    cell = lax.broadcasted_iota(jnp.int32, (SUB, lanes), 1)

    def spread(group, which):
        return jnp.broadcast_to(coef[group, :, which : which + 1], (SUB, lanes))

    def build(n, carry):
        q = n // PACK
        k = n % PACK
        level = spread(n, 0)
        for r in range(deep):
            line = [jnp.broadcast_to(base[0, i, r : r + 1, :], (SUB, lanes)) for i in range(4)]
            fe[q, 1 + k, r] = jnp.where(line[1] > level, line[0], 0.0)
            fn[q, 1 + k, r] = jnp.where(line[3] > level, line[2], 0.0)
        return carry

    lax.fori_loop(0, quads * PACK, build, 0)

    def build_strip(q, carry):
        level = spread(q * PACK, 0)
        for k in range(1, PACK):
            level = jnp.where(cell >= STRIDE * k, spread(q * PACK + k, 0), level)
        for r in range(deep):
            line = [jnp.broadcast_to(base[1, i, r : r + 1, :], (SUB, lanes)) for i in range(4)]
            fe[q, 0, r] = jnp.where(line[1] > level, line[0], 0.0)
            fn[q, 0, r] = jnp.where(line[3] > level, line[2], 0.0)
        return carry

    lax.fori_loop(0, quads, build_strip, 0)

    own.wait()
    for copy in obs:
        copy.wait()
    arrived = rcv[...].reshape(slots, width)
    for i, part in enumerate(split3(arrived.T[: parts.shape[1]])):
        parts[i] = part
    columns = arrived[:, total + 1 : total + 2]
    lines = arrived[:, total + 2 : total + 3]
    places = lax.broadcasted_iota(jnp.int32, (slots, lanes), 1).astype(jnp.float32)
    table[...] = jnp.where(columns == places, 1.0, 0.0)

    def scatter(r, carry):
        at_row = jnp.where(lines == r.astype(jnp.float32), table[...], 0.0).astype(jnp.bfloat16)
        cells = jnp.zeros((parts.shape[1], lanes), jnp.float32)
        for i in range(3):
            cells = cells + jnp.dot(parts[i], at_row, preferred_element_type=jnp.float32)
        count = jnp.broadcast_to(cells[total : total + 1], (SUB, lanes))
        depth = jnp.broadcast_to(maps[2, pl.ds(r, 1), :], (SUB, lanes))
        for n in range(quads * PACK):
            wet = depth > spread(n, 0)
            block = cells[SUB * n : SUB * n + SUB]
            f[n // PACK, 1 + n % PACK, PASSES + r] = jnp.where(wet, spread(n, 1) * block, 0.0)
            gain[n // PACK, n % PACK, r] = jnp.where(wet, spread(n, 2) * count, 0.0)
        return carry

    lax.fori_loop(0, rows, scatter, 0)

    group_of, inside = cell // STRIDE, cell % STRIDE

    def strip_row(q, r):
        z = zero
        for k in range(PACK):
            moved = pltpu.roll(f[q, 1 + k, r], (STRIDE * k + OWN) % lanes, 1)
            z = moved if k == 0 else jnp.where(group_of == k, moved, z)
        x = jnp.where(inside < EAST, pltpu.roll(z, lanes - PASSES, 1), pltpu.roll(z, EAST, 1))
        return z, x

    def halo(par, q, d):
        dl, db = ways[d]
        send, recv = halo_send.at[par, q, d], halo_recv.at[par, q, d]
        to_lat = {-1: rows + PASSES, 1: 0}
        if dl == 0:
            first = PASSES if db < 0 else last - PASSES
            src = f.at[q, pl.ds(1, PACK), pl.ds(first, PASSES)]
            dst = (hn if db < 0 else hs).at[par, q]
        else:
            pack, target = (0, pe) if dl < 0 else (1, pw)
            if db == 0:
                src = pk.at[q, pack]
                dst = target.at[par, q, pl.ds(1, 3)]
            else:
                src = pk.at[q, pack, pl.ds(0 if db < 0 else 2, 1)]
                dst = target.at[par, q, pl.ds(4 if db < 0 else 0, 1)]
        return remote(src, dst, send, recv, at(dl, db))

    def emit(par, q):
        for d in (0, 1):
            only(there[ways[d][1]], lambda d=d: halo(par, q, d).start())
        packs = {}
        for r in range(PASSES, last):
            z, x = strip_row(q, r)
            f[q, 0, r] = x
            a, j = place_of(r, rows)
            for side, first in ((0, OWN), (1, PASSES)):
                moved = pltpu.roll(z, (PASSES * j - first) % lanes, 1)
                if j:
                    moved = jnp.where(inside >= PASSES * j, moved, packs[side])
                packs[side] = moved
                pk[q, side, a - 1] = moved
        for d in (6, 7, 4, 5, 2, 3):
            only(there[ways[d][1]], lambda d=d: halo(par, q, d).start())

    def first_emit(q, carry):
        emit(0, q)
        return carry

    lax.fori_loop(0, quads, first_emit, 0)

    def passes(q, p):
        v = [f[q, p, r] for r in range(deep)]
        for t in range(PASSES):
            new = list(v)
            south = fn[q, p, t] * (v[t + 1] - v[t])
            for r in range(t + 1, deep - 1 - t):
                centre = v[r]
                flux = fe[q, p, r] * (pltpu.roll(centre, lanes - 1, 1) - centre)
                north = fn[q, p, r] * (v[r + 1] - centre)
                change = (flux - pltpu.roll(flux, 1, 1)) + (north - south)
                new[r] = centre + change
                south = north
            v = new
        for r in range(PASSES, last):
            res[p, r - PASSES] = v[r]

    def reduce_lat(k):
        return remote(red, red_lat.at[lat], sum_send.at[k], sum_recv.at[k], beside[k])

    def reduce_lon(k):
        n = len(beside) + k
        return remote(red, red_lon.at[lon], sum_send.at[n], sum_recv.at[n], along[k])

    def stage(e, carry):
        par = lax.rem(e, 2)
        odd = par == 1

        def quad(q, carry):
            for d in range(8):
                only(there[-ways[d][1]], lambda d=d: halo(par, q, d).wait_recv())
            for i in range(PASSES):
                for k in range(PACK):
                    f[q, 1 + k, i] = hs[par, q, k, i]
                    f[q, 1 + k, last + i] = hn[par, q, k, i]
            for r in range(deep):
                if PASSES <= r < last:
                    x = f[q, 0, r]
                else:
                    x = strip_row(q, r)[1]
                a, j = place_of(r, rows)
                west = pltpu.roll(pw[par, q, a], (-PASSES * j) % lanes, 1)
                east = pltpu.roll(pe[par, q, a], (EAST + OWN - PASSES * j) % lanes, 1)
                x = jnp.where(inside < PASSES, west, x)
                x = jnp.where((inside >= EAST + OWN) & (inside < EAST + OWN + PASSES), east, x)
                f[q, 0, r] = x

            def plane(p, carry):
                passes(q, p)
                return carry

            lax.fori_loop(0, 1 + PACK, plane, 0)
            for d in range(8):
                only(there[ways[d][1]], lambda d=d: halo(par, q, d).wait_send())
            sums = mom[e]
            for r in range(rows):
                edge = res[0, r]
                edge = jnp.where(
                    inside < PASSES, pltpu.roll(edge, lanes - EAST - PASSES, 1), edge
                )
                for k in range(PACK):
                    moved = pltpu.roll(edge, lanes - PASSES - STRIDE * k, 1)
                    fixed = jnp.where(
                        (cell < PASSES) | (cell >= lanes - PASSES), moved, res[1 + k, r]
                    )
                    weighed = fixed * jnp.where(odd, gain[q, k, r], 1.0)
                    sums = sums + fixed * weighed
                    f[q, 1 + k, PASSES + r] = weighed
            mom[e] = sums

            @pl.when(jnp.logical_not(odd))
            def _():
                for r in range(rows):
                    for k in range(PACK):
                        first = (q * PACK + k) * (SUB * rows) + r
                        v_out[lax.div(e, 2), pl.ds(first, SUB, stride=rows), :] = f[
                            q, 1 + k, PASSES + r
                        ]

            @pl.when(e < STAGES - 1)
            def _():
                emit(1 - par, q)

            return carry

        lax.fori_loop(0, quads, quad, 0)

        @pl.when(e == STAGES - 2)
        def _():
            for i in range(4):
                red[i : i + 1, :] = jnp.sum(mom[i], 0, keepdims=True)
            red_lat[lat] = red[...]
            for k in range(len(beside)):
                reduce_lat(k).start()

        return carry

    lax.fori_loop(0, STAGES, stage, 0)

    for k in range(len(beside)):
        reduce_lat(k).wait()
    red[...] = jnp.sum(red_lat[...], 0)
    red_lon[lon] = red[...]
    for k in range(len(along)):
        reduce_lon(k).start()
    for k in range(len(along)):
        reduce_lon(k).wait()
    sums = jnp.sum(jnp.sum(red_lon[...], 0), 1, keepdims=True)
    m0 = sums[0:1]
    x, y, z = sums[1:2] / m0, sums[2:3] / m0, sums[3:4] / m0
    alpha = 1.0 / (1.0 + x)
    beta = (y - x * x) * alpha * alpha
    c0, c1 = 1.0 - alpha + beta, -alpha
    curve = c0 * c0 * (1.0 + x) + 2.0 * c0 * c1 * (x + y) + c1 * c1 * (y + z)
    second = beta / curve
    values = (
        alpha + second * c0,
        second * c1,
        (1.0 - second) * (1.0 - alpha) - second * beta,
        -(1.0 - second) * alpha - second * c0,
        alpha * second,
    )
    for i, value in enumerate(values):
        c_out[i : i + 1, :] = jnp.broadcast_to(value, (1, lanes))


def combine_kernel(v, c, increment, residual):
    shape = increment.shape

    def scalar(i):
        return jnp.broadcast_to(c[i : i + 1, :].reshape(1, 1, shape[2]), shape)

    increment[...] = scalar(0) * v[0] + scalar(1) * v[1]
    residual[...] = scalar(2) * v[0] + scalar(3) * v[1] + scalar(4) * v[2]


def local(
    kappa_east, kappa_north, depth, sigma, obs_precision, obs_tile, obs_col, obs_lat, innovation
):
    rows, lanes = kappa_east.shape
    total = sigma.shape[0]
    tiles, bands = lax.axis_size("lon"), lax.axis_size("lat")
    listed = obs_col.shape[0]
    cap = 2 * listed // tiles
    quads = -(-total // (SUB * PACK))
    channels = quads * PACK * SUB
    levels = (total - 1) // 2
    width = -(-(total + 3) // 128) * 128

    data = jnp.concatenate(
        [
            innovation,
            jnp.zeros((width - total, listed), jnp.float32),
        ]
    )
    row = lax.broadcasted_iota(jnp.int32, (width, listed), 0)
    data = jnp.where(row == total, 1.0, data)
    data = jnp.where(row == total + 1, obs_col.astype(jnp.float32)[None], data)
    data = jnp.where(row == total + 2, obs_lat.astype(jnp.float32)[None], data)
    maps = jnp.stack([kappa_east, kappa_north, depth.astype(jnp.float32)])
    ids = jnp.arange(channels, dtype=jnp.int32)
    level = jnp.where(ids < 2 * levels, ids % levels, 0)
    level = jnp.where(ids < total, level, 2 * levels).astype(jnp.float32)
    scale = jnp.pad(sigma, (0, channels - total))
    weight = jnp.pad(obs_precision, (0, channels - total))
    coef = jnp.stack([level, scale * weight, scale * scale * weight, scale], axis=-1)
    coef = coef.reshape(quads * PACK, SUB, 4)

    deep = rows + 2 * PASSES
    padded = -(-deep // SUB) * SUB + SUB
    vmem = pl.BlockSpec(memory_space=pltpu.VMEM)
    f32 = jnp.float32
    dma = pltpu.SemaphoreType.DMA
    planes = (quads, 1 + PACK, deep, SUB, lanes)
    slots = tiles * cap
    v, c = pl.pallas_call(
        functools.partial(main_kernel, tiles, bands, cap, total),
        out_shape=[
            jax.ShapeDtypeStruct((3, channels * rows, lanes), f32),
            jax.ShapeDtypeStruct((SUB, lanes), f32),
        ],
        in_specs=[vmem] * 5,
        out_specs=[vmem] * 2,
        scratch_shapes=[
            pltpu.VMEM((tiles, cap, width), f32),
            pltpu.VMEM((tiles, cap, width), f32),
            pltpu.VMEM((3, channels, slots), jnp.bfloat16),
            pltpu.VMEM((slots, lanes), f32),
            pltpu.VMEM((9, 3, rows, lanes), f32),
            pltpu.VMEM((3, 3, padded, lanes), f32),
            pltpu.VMEM((3, padded, lanes), f32),
            pltpu.VMEM((2, 4, padded - SUB, lanes), f32),
            pltpu.VMEM(planes, f32),
            pltpu.VMEM(planes, f32),
            pltpu.VMEM(planes, f32),
            pltpu.VMEM((1 + PACK, rows, SUB, lanes), f32),
            pltpu.VMEM((quads, PACK, rows, SUB, lanes), f32),
            pltpu.VMEM((2, quads, PACK, PASSES, SUB, lanes), f32),
            pltpu.VMEM((2, quads, PACK, PASSES, SUB, lanes), f32),
            pltpu.VMEM((2, quads, 5, SUB, lanes), f32),
            pltpu.VMEM((2, quads, 5, SUB, lanes), f32),
            pltpu.VMEM((quads, 2, 3, SUB, lanes), f32),
            pltpu.VMEM((STAGES, SUB, lanes), f32),
            pltpu.VMEM((SUB, lanes), f32),
            pltpu.VMEM((bands, SUB, lanes), f32),
            pltpu.VMEM((tiles, SUB, lanes), f32),
            dma((tiles - 1,)),
            dma((tiles - 1,)),
            dma((8,)),
            dma((8,)),
            dma,
            dma((2, quads, 8)),
            dma((2, quads, 8)),
            dma((tiles + bands - 2,)),
            dma((tiles + bands - 2,)),
        ],
        compiler_params=pltpu.CompilerParams(
            collective_id=1, has_side_effects=True, vmem_limit_bytes=40 * 1024 * 1024
        ),
        name="smooth_all",
    )(data, obs_tile.reshape(1, listed), obs_tile, maps, coef)

    v = v.reshape(3, channels, rows, lanes)
    block = SUB * PACK
    out = pl.BlockSpec((block, rows, lanes), lambda i: (i, 0, 0))
    return pl.pallas_call(
        combine_kernel,
        grid=(quads,),
        out_shape=[jax.ShapeDtypeStruct((total, rows, lanes), f32)] * 2,
        in_specs=[
            pl.BlockSpec((3, block, rows, lanes), lambda i: (0, i, 0, 0)),
            pl.BlockSpec((SUB, lanes), lambda i: (0, 0)),
        ],
        out_specs=[out, out],
        name="combine",
    )(v, c)


def solution(mesh):
    return jax.shard_map(
        local,
        mesh=mesh,
        in_specs=(
            P("lat", "lon"),
            P("lat", "lon"),
            P("lat", "lon"),
            P(),
            P(),
            P(("lon", "lat"), None),
            P(("lon", "lat")),
            P(("lon", "lat")),
            P(None, ("lon", "lat")),
        ),
        out_specs=(P(None, "lat", "lon"), P(None, "lat", "lon")),
        check_vma=False,
    )
```

profile of v0, /device:TPU:0, one launch (start us, length us, event | category | flops | bytes accessed | tf_op | source)
XLA Modules:
  0.0 154.4 jit_solution(7869271660512443080)
XLA Ops:
  0.6 0.7 convert_element_type.24
  1.3 0.7 convert_element_type.23
  2.0 0.7 pad_multiply_fusion
  2.7 0.7 convert_bitcast_fusion
  3.4 0.7 pad_maximum_fusion.1.maps
  4.1 0.8 copy.24.tile_col
  4.8 0.2 stack.33
  5.0 0.2 stack.34
  5.2 0.2 stack.35
  5.5 0.1 pad_maximum_fusion.coef
  5.6 1.1 select_select_fusion.data
  6.7 0.0 copy-start.2
  6.7 0.6 copy-done.2
  7.4 139.5 %smooth_all.1 = (f32[3,2560,128]{2,1,0:T(8,128)S(1)}, f32[8,128]{1,0:T(8,128)S(1)}) custom-call(f32[256,128]{1,0:T(8,128)S(1)} %select_select_fusion.data, s32[1,128]{1,0:T(1,128)S(1)} %bitcast.7, s32[128,1]{1,0:T(8,128)S(1)} %copy.24.tile_col, f32[3,16,128]{2,1,0:T(8,128)S(1)} %pad_maximum_fusion.1.maps, f32[20,8,4]{2,1,0:T(8,128)S(1)} %pad_maximum_fusion.coef), custom_call_target="tpu_custom_call" | custom-call | tf_op jit(solution)/shard_map/smooth_all/pallas_call | solution.py:512
  146.9 0.0 copy-start
  146.9 1.9 %copy-done = f32[3,2560,128]{2,1,0:T(8,128)} copy-done((f32[3,2560,128]{2,1,0:T(8,128)}, f32[3,2560,128]{2,1,0:T(8,128)S(1)}, u32[]{:S(2)}) %copy-start) | copy-done | bytes 3932184
  148.7 0.0 copy-start.1
  148.7 0.6 copy-done.1
  149.3 5.1 %combine.1 = (f32[151,16,128]{2,1,0:T(8,128)}, f32[151,16,128]{2,1,0:T(8,128)}) custom-call(f32[3,160,16,128]{3,2,1,0:T(8,128)} %bitcast.6, f32[8,128]{1,0:T(8,128)} %copy-done.1), custom_call_target="tpu_custom_call" | custom-call | tf_op jit(solution)/shard_map/combine/pallas_call | solution.py:562
  (3 shorter events, 0.1 us)
Async XLA Ops:
  6.7 0.7 copy-start.2
  146.9 1.9 %copy-start = (f32[3,2560,128]{2,1,0:T(8,128)}, f32[3,2560,128]{2,1,0:T(8,128)S(1)}, u32[]{:S(2)}) copy-start(f32[3,2560,128]{2,1,0:T(8,128)S(1)} %get-tuple-element.4) | copy-start | bytes 11796484
  148.7 0.6 copy-start.1
where the time goes:
time: 155 us; the launch traced here: 154 us
  Pallas kernels  145 us (94%)
  other arithmetic  4.67 us (3%)
  local copies, waits for them, and re-layouts  4.47 us (3%)
    pallas_call x1, Pallas kernels, local(): pl.pallas_call(functools.partial(main_kernel, tiles, bands, cap, total),...  140 us
    pallas_call x1, Pallas kernels, local(): pl.pallas_call(combine_kernel, grid=(quads,), out_shape=[jax.ShapeDtypeSt...  5.11 us
    unnamed x7, local copies, waits for them, and re-layouts  3.86 us

commit v1 on v0

v1 whole, which is shorter than its diff:
```python
import functools

import jax
import jax.numpy as jnp
from jax import lax
from jax.experimental import pallas as pl
from jax.experimental.pallas import tpu as pltpu
from jax.sharding import PartitionSpec as P

MESH = pl.DeviceIdType.MESH
SUB = 8
GROUPS = 4
PASSES = 5
STAGES = 5
EDGE = 8


def split3(x):
    high = x.astype(jnp.bfloat16)
    left = x - high.astype(jnp.float32)
    middle = left.astype(jnp.bfloat16)
    low = (left - middle.astype(jnp.float32)).astype(jnp.bfloat16)
    return high, middle, low


def chunks(first, end, most=8):
    count = -(-(end - first) // most)
    cuts = [first + (end - first) * i // count for i in range(count + 1)]
    return list(zip(cuts[:-1], cuts[1:]))


def iota(shape, dim):
    return lax.broadcasted_iota(jnp.int32, shape, dim)


def ones_where(mask):
    return jnp.where(mask, 1.0, 0.0).astype(jnp.bfloat16)


def main_kernel(
    tiles,
    bands,
    cap,
    total,
    data,
    tile_row,
    tile_col,
    maps,
    coef,
    v_out,
    c_out,
    pay,
    rcv,
    values,
    near,
    ext,
    base,
    f,
    fe,
    fn,
    tmp,
    gain,
    hs,
    hn,
    pw,
    pe,
    pk,
    mom,
    red,
    red_lat,
    red_lon,
    obs_send,
    obs_recv,
    map_send,
    map_recv,
    own_sem,
    halo_send,
    halo_recv,
    sum_send,
    sum_recv,
):
    lon, lat = lax.axis_index("lon"), lax.axis_index("lat")
    rows, lanes = maps.shape[1], maps.shape[2]
    blocks = f.shape[0]
    deep = rows + 2 * PASSES
    last = rows + PASSES
    wide = lanes // GROUPS
    span = wide + 2 * EDGE
    regs = span // SUB
    has_s, has_n = lat > 0, lat < bands - 1

    def at(dl, db):
        return lax.rem(lon + dl + tiles, tiles), lax.rem(lat + db + bands, bands)

    beside = [(lon, lax.rem(lat + k, bands)) for k in range(1, bands)]
    along = [(lax.rem(lon + k, tiles), lat) for k in range(1, tiles)]
    ways = [(0, -1), (0, 1), (-1, 0), (1, 0), (-1, -1), (1, -1), (-1, 1), (1, 1)]
    there = {-1: has_s, 0: None, 1: has_n}

    def only(cond, body):
        if cond is None:
            body()
        else:
            pl.when(cond)(body)

    barrier = pltpu.get_barrier_semaphore()

    def greet(peer):
        pl.semaphore_signal(barrier, inc=1, device_id=peer, device_id_type=MESH)

    for peer in beside + along:
        greet(peer)
    for dl, db in ways[4:]:
        only(there[db], functools.partial(greet, at(dl, db)))

    def remote(src, dst, send, recv, peer):
        return pltpu.make_async_remote_copy(
            src_ref=src,
            dst_ref=dst,
            send_sem=send,
            recv_sem=recv,
            device_id=peer,
            device_id_type=MESH,
        )

    listed = tile_row.shape[1]
    slots = tiles * cap
    same = tile_col[...] == tile_row[...]
    earlier = iota((listed, listed), 0) < iota((listed, listed), 1)
    rank = jnp.sum(jnp.where(same & earlier, 1.0, 0.0), 0, keepdims=True)
    slot = tile_row[...] * cap + rank.astype(jnp.int32)
    chosen = ones_where(iota((slots, listed), 0) == slot)
    width = data.shape[0]
    packed = jnp.zeros((slots, width), jnp.float32)
    for part in split3(data[...]):
        packed = packed + lax.dot_general(
            chosen, part, (((1,), (1,)), ((), ())), preferred_element_type=jnp.float32
        )
    pay[...] = packed.reshape(tiles, cap, width)

    diagonal = jnp.where(has_s, 2, 0) + jnp.where(has_n, 2, 0)
    pl.semaphore_wait(barrier, len(beside) + len(along) + diagonal)

    def slot_of(dl, db):
        return (dl + 1) * 3 + db + 1

    def map_copy(d):
        dl, db = ways[d]
        return remote(
            maps, near.at[slot_of(-dl, -db)], map_send.at[d], map_recv.at[d], at(dl, db)
        )

    for d in (4, 5, 6, 7, 2, 3, 0, 1):
        only(there[ways[d][1]], lambda d=d: map_copy(d).start())
    obs = []
    for k, peer in enumerate(along):
        copy = remote(pay.at[peer[0]], rcv.at[lon], obs_send.at[k], obs_recv.at[k], peer)
        copy.start()
        obs.append(copy)
    own = pltpu.make_async_copy(pay.at[lon], rcv.at[lon], own_sem)
    own.start()

    nothing = jnp.zeros(maps.shape, jnp.float32)
    near[slot_of(0, 0)] = maps[...]
    corner = jnp.zeros(pw.shape[:2] + pw.shape[3:], jnp.float32)

    @pl.when(jnp.logical_not(has_s))
    def _():
        for dl in (-1, 0, 1):
            near[slot_of(dl, -1)] = nothing
        hs[...] = jnp.zeros(hs.shape, jnp.float32)
        pw[:, :, 0] = corner
        pe[:, :, 0] = corner

    @pl.when(jnp.logical_not(has_n))
    def _():
        for dl in (-1, 0, 1):
            near[slot_of(dl, 1)] = nothing
        hn[...] = jnp.zeros(hn.shape, jnp.float32)
        pw[:, :, pw.shape[2] - 1] = corner
        pe[:, :, pe.shape[2] - 1] = corner

    mom[...] = jnp.zeros(mom.shape, jnp.float32)
    red[...] = jnp.zeros(red.shape, jnp.float32)
    ext[...] = jnp.zeros(ext.shape, jnp.float32)

    def clear(b, carry):
        for r in (0, deep - 1):
            f[b, r] = jnp.zeros((span, lanes), jnp.float32)
        for c in (0, span - EDGE):
            f[b, :, c : c + EDGE] = jnp.zeros((deep, EDGE, lanes), jnp.float32)
            gain[b, :, c : c + EDGE] = jnp.zeros((rows, EDGE, lanes), jnp.float32)
        return carry

    lax.fori_loop(0, blocks, clear, 0)

    for d in range(8):
        dl, db = ways[d]
        only(there[-db], lambda d=d: map_copy(d).wait_recv())
    for d in range(8):
        only(there[ways[d][1]], lambda d=d: map_copy(d).wait_send())

    for m in range(3):
        for side in range(3):
            ext[m, side, 0:PASSES] = near[3 * side, m, rows - PASSES : rows]
            ext[m, side, PASSES:last] = near[3 * side + 1, m]
            ext[m, side, last:deep] = near[3 * side + 2, m, 0:PASSES]
    edge = iota((deep, lanes), 1) == lanes - 1
    east, north, depth = [], [], [ext[2, side, 0:deep] for side in range(3)]
    ahead = [pltpu.roll(ext[2, side], lanes - 1, 1)[0:deep] for side in range(3)]
    for side in range(3):
        moved = ahead[side]
        if side < 2:
            moved = jnp.where(edge, ahead[side + 1], moved)
        east.append(jnp.minimum(depth[side], moved))
        north.append(jnp.minimum(depth[side], ext[2, side, 1 : deep + 1]))
    reach = 3 * lanes
    column = iota((reach, regs * lanes), 0) - lanes + EDGE
    target = iota((reach, regs * lanes), 1)
    start = target % lanes // wide * wide + target // lanes * SUB
    to_lane = ones_where((column >= start) & (column < start + SUB))
    sub_mask = iota((1, SUB, reach), 2) % SUB == iota((1, SUB, reach), 1)
    kinds = (
        [ext[0, side, 0:deep] for side in range(3)],
        east,
        [ext[1, side, 0:deep] for side in range(3)],
        north,
        depth,
    )
    for m, kind in enumerate(kinds):
        line = jnp.concatenate(kind, 1)
        parts = [line] if m in (1, 3, 4) else [x.astype(jnp.float32) for x in split3(line)]
        out = jnp.zeros((deep * SUB, regs * lanes), jnp.float32)
        for part in parts:
            picked = jnp.where(sub_mask, part[:, None, :], 0.0).reshape(deep * SUB, reach)
            out = out + jnp.dot(
                picked.astype(jnp.bfloat16), to_lane, preferred_element_type=jnp.float32
            )
        for i in range(regs):
            base[m, :, SUB * i : SUB * i + SUB] = out[:, lanes * i : lanes * i + lanes].reshape(
                deep, SUB, lanes
            )

    def build(b, carry):
        level = coef[b, 0:1][None]
        for j in range(regs):
            pick = pl.ds(j, SUB, stride=regs)
            for r in range(deep):
                fe[b, j, r] = jnp.where(base[1, r, pick, :] > level[0], base[0, r, pick, :], 0.0)
                fn[b, j, r] = jnp.where(base[3, r, pick, :] > level[0], base[2, r, pick, :], 0.0)
        return carry

    lax.fori_loop(0, blocks, build, 0)

    own.wait()
    for copy in obs:
        copy.wait()
    arrived = rcv[...].reshape(slots, width)
    columns = arrived[:, total + 1 : total + 2]
    flat = (blocks + 1) * lanes
    source, goal = iota((width, flat), 0), iota((width, flat), 1)
    channel = jnp.where(goal < blocks * lanes, goal // lanes * wide + goal % wide, total)
    to_flat = ones_where(source == channel)
    group = (iota((slots, flat), 1) % lanes // wide * wide).astype(jnp.float32)
    mine = (columns >= group) & (columns < group + wide)
    for i, part in enumerate(split3(arrived)):
        wide_part = jnp.dot(part, to_flat, preferred_element_type=jnp.float32)
        values[i] = jnp.where(mine, wide_part, 0.0).astype(jnp.bfloat16)
    picker = ones_where(iota((SUB, width), 1) == iota((SUB, width), 0) + total + 1)
    turned = lax.dot_general(
        picker,
        arrived.astype(jnp.bfloat16),
        (((1,), (1,)), ((), ())),
        preferred_element_type=jnp.float32,
    )
    place = turned[1:2] * wide + turned[0:1] - jnp.floor(turned[0:1] / wide) * wide
    spots = iota((rows * wide, slots), 0).astype(jnp.float32)
    to_cell = ones_where(spots == place)
    own_cols = slice(EDGE, EDGE + wide)
    depths = base[4, PASSES:last, own_cols]

    def cells_of(b):
        out = jnp.zeros((rows * wide, lanes), jnp.float32)
        for i in range(3):
            out = out + jnp.dot(
                to_cell,
                values[i, :, b * lanes : (b + 1) * lanes],
                preferred_element_type=jnp.float32,
            )
        return out.reshape(rows, wide, lanes)

    counts = cells_of(blocks)
    for b in range(blocks):
        wet = depths > coef[b, 0:1][None]
        f[b, PASSES:last, own_cols] = jnp.where(wet, coef[b, 1:2][None] * cells_of(b), 0.0)
        gain[b, :, own_cols] = jnp.where(wet, coef[b, 2:3][None] * counts, 0.0)

    lane = iota((SUB, lanes), 1)
    subs = iota((SUB, lanes), 0)
    packs = rows // GROUPS
    inner = pl.ds(EDGE, wide)

    def halo(par, b, d):
        dl, db = ways[d]
        send, recv = halo_send.at[par, b, d], halo_recv.at[par, b, d]
        if dl == 0:
            first = PASSES if db < 0 else last - PASSES
            src = f.at[b, pl.ds(first, PASSES), inner]
            dst = (hn if db < 0 else hs).at[par, b]
        else:
            pack, to = (0, pe) if dl < 0 else (1, pw)
            if db == 0:
                src = pk.at[b, pack]
                dst = to.at[par, b, pl.ds(1, packs)]
            else:
                src = pk.at[b, pack, pl.ds(0 if db < 0 else packs - 1, 1)]
                dst = to.at[par, b, pl.ds(packs + 1 if db < 0 else 0, 1)]
        return remote(src, dst, send, recv, at(dl, db))

    def emit(par, b):
        for d in (0, 1):
            only(there[ways[d][1]], lambda d=d: halo(par, b, d).start())
        for a in range(packs):
            for side, first, from_lane in ((0, EDGE, 0), (1, wide, lanes - wide)):
                out = None
                for i in range(GROUPS):
                    piece = f[b, PASSES + GROUPS * a + i, first : first + EDGE]
                    move = (wide * i - from_lane) % lanes
                    piece = pltpu.roll(piece, move, 1) if move else piece
                    out = piece if out is None else jnp.where(lane >= wide * i, piece, out)
                pk[b, side, a] = out
        for d in (6, 7, 4, 5, 2, 3):
            only(there[ways[d][1]], lambda d=d: halo(par, b, d).start())

    def first_emit(b, carry):
        emit(0, b)
        return carry

    lax.fori_loop(0, blocks, first_emit, 0)

    def reduce_lat(k):
        return remote(red, red_lat.at[lat], sum_send.at[k], sum_recv.at[k], beside[k])

    def reduce_lon(k):
        n = len(beside) + k
        return remote(red, red_lon.at[lon], sum_send.at[n], sum_recv.at[n], along[k])

    def one_pass(b, t, finish):
        def old(j, lo, hi):
            if t == 0:
                return jnp.stack(
                    [f[b, r, pl.ds(j, SUB, stride=regs), :] for r in range(lo, hi)]
                )
            return tmp[(t + 1) % 2, j, lo:hi]

        for lo, hi in chunks(t + 1, deep - 1 - t):
            v = old(0, lo - 1, hi + 1)
            wrap = pltpu.roll(v[1:-1], SUB - 1, 1)
            end = old(regs - 1, lo, hi)
            end = fe[b, regs - 1, lo:hi] * (wrap - end)
            west = pltpu.roll(end, 1, 1)
            for j in range(regs):
                centre = v[1:-1]
                if j < regs - 1:
                    following = old(j + 1, lo - 1, hi + 1)
                    flux = fe[b, j, lo:hi] * (following[1:-1] - centre)
                else:
                    following, flux = None, end
                up = fn[b, j, lo - 1 : hi] * (v[1:] - v[:-1])
                new = centre + ((flux - west) + (up[1:] - up[:-1]))
                if finish is None:
                    tmp[t % 2, j, lo:hi] = new
                else:
                    finish(j, lo, new)
                v, west = following, flux

    def stage(e, carry):
        par = lax.rem(e, 2)
        odd = par == 1

        def block(b, carry):
            for d in range(8):
                only(there[-ways[d][1]], lambda d=d: halo(par, b, d).wait_recv())
            f[b, 0:PASSES, own_cols] = hs[par, b]
            f[b, last:deep, own_cols] = hn[par, b]
            for r in range(1, deep - 1):
                a, i = (r - 1) // GROUPS, (r - 1) % GROUPS
                west = pltpu.roll(f[b, r, wide : wide + EDGE], wide, 1)
                far = pw[par, b, a]
                far = pltpu.roll(far, lanes - wide * i, 1) if i else far
                f[b, r, 0:EDGE] = jnp.where(lane < wide, far, west)
                east = pltpu.roll(f[b, r, EDGE : 2 * EDGE], lanes - wide, 1)
                far = pe[par, b, a]
                move = (lanes - wide - wide * i) % lanes
                far = pltpu.roll(far, move, 1) if move else far
                f[b, r, wide + EDGE : span] = jnp.where(lane >= lanes - wide, far, east)
            for t in range(PASSES - 1):
                one_pass(b, t, None)
            for d in range(8):
                only(there[ways[d][1]], lambda d=d: halo(par, b, d).wait_send())

            def finish(j, lo, new):
                pick = pl.ds(j, SUB, stride=regs)
                at_col = subs * regs + j
                own_here = jnp.where((at_col >= EDGE) & (at_col < EDGE + wide), 1.0, 0.0)
                sums = mom[e]
                for i in range(new.shape[0]):
                    r = lo + i
                    weight = jnp.where(odd, gain[b, r - PASSES, pick, :], own_here)
                    weighed = new[i] * weight
                    sums = sums + new[i] * weighed
                    f[b, r, pick, :] = weighed
                mom[e] = sums

            one_pass(b, PASSES - 1, finish)

            @pl.when(e < STAGES - 1)
            def _():
                emit(1 - par, b)

            @pl.when(jnp.logical_not(odd))
            def _():
                for a in range(packs):
                    first = PASSES + GROUPS * a
                    square = f[b, first : first + GROUPS, own_cols].reshape(lanes, lanes).T
                    for i in range(GROUPS):
                        out = None
                        for g in range(GROUPS):
                            piece = square[wide * g : wide * g + wide]
                            move = wide * (g - i) % lanes
                            piece = pltpu.roll(piece, move, 1) if move else piece
                            lane_all = iota((wide, lanes), 1)
                            out = piece if g == 0 else jnp.where(lane_all >= wide * g, piece, out)
                        begin = b * (wide * rows) + GROUPS * a + i
                        v_out[lax.div(e, 2), pl.ds(begin, wide, stride=rows), :] = out

            @pl.when((e == STAGES - 1) & (b == blocks // 2))
            def _():
                for k in range(len(beside)):
                    reduce_lat(k).wait()
                red[...] = jnp.sum(red_lat[...], 0)
                red_lon[lon] = red[...]
                for k in range(len(along)):
                    reduce_lon(k).start()

            return carry

        lax.fori_loop(0, blocks, block, 0)

        @pl.when(e == STAGES - 2)
        def _():
            for i in range(4):
                red[i : i + 1, :] = jnp.sum(mom[i], 0, keepdims=True)
            red_lat[lat] = red[...]
            for k in range(len(beside)):
                reduce_lat(k).start()

        return carry

    lax.fori_loop(0, STAGES, stage, 0)

    for k in range(len(along)):
        reduce_lon(k).wait()
    sums = jnp.sum(jnp.sum(red_lon[...], 0), 1, keepdims=True)
    m0 = sums[0:1]
    x, y, z = sums[1:2] / m0, sums[2:3] / m0, sums[3:4] / m0
    alpha = 1.0 / (1.0 + x)
    beta = (y - x * x) * alpha * alpha
    c0, c1 = 1.0 - alpha + beta, -alpha
    curve = c0 * c0 * (1.0 + x) + 2.0 * c0 * c1 * (x + y) + c1 * c1 * (y + z)
    second = beta / curve
    values = (
        alpha + second * c0,
        second * c1,
        (1.0 - second) * (1.0 - alpha) - second * beta,
        -(1.0 - second) * alpha - second * c0,
        alpha * second,
    )
    for i, value in enumerate(values):
        c_out[i : i + 1, :] = jnp.broadcast_to(value, (1, lanes))


def combine_kernel(v, c, increment, residual):
    shape = increment.shape

    def scalar(i):
        return jnp.broadcast_to(c[i : i + 1, :].reshape(1, 1, shape[2]), shape)

    increment[...] = scalar(0) * v[0] + scalar(1) * v[1]
    residual[...] = scalar(2) * v[0] + scalar(3) * v[1] + scalar(4) * v[2]


def local(
    kappa_east, kappa_north, depth, sigma, obs_precision, obs_tile, obs_col, obs_lat, innovation
):
    rows, lanes = kappa_east.shape
    total = sigma.shape[0]
    tiles, bands = lax.axis_size("lon"), lax.axis_size("lat")
    listed = obs_col.shape[0]
    cap = 2 * listed // tiles
    wide = lanes // GROUPS
    blocks = -(-total // wide)
    channels = blocks * wide
    levels = (total - 1) // 2
    width = -(-(total + 3) // 128) * 128

    data = jnp.concatenate(
        [
            innovation,
            jnp.zeros((width - total, listed), jnp.float32),
        ]
    )
    row = lax.broadcasted_iota(jnp.int32, (width, listed), 0)
    data = jnp.where(row == total, 1.0, data)
    data = jnp.where(row == total + 1, obs_col.astype(jnp.float32)[None], data)
    data = jnp.where(row == total + 2, obs_lat.astype(jnp.float32)[None], data)
    maps = jnp.stack([kappa_east, kappa_north, depth.astype(jnp.float32)])
    ids = jnp.arange(channels, dtype=jnp.int32)
    level = jnp.where(ids < 2 * levels, ids % levels, 0)
    level = jnp.where(ids < total, level, 2 * levels).astype(jnp.float32)
    scale = jnp.pad(sigma, (0, channels - total))
    weight = jnp.pad(obs_precision, (0, channels - total))
    coef = jnp.stack([level, scale * weight, scale * scale * weight])
    coef = jnp.tile(coef.reshape(3, blocks, wide), (1, 1, GROUPS)).transpose(1, 0, 2)
    coef = jnp.pad(coef, ((0, 0), (0, SUB - 3), (0, 0)))

    deep = rows + 2 * PASSES
    span = wide + 2 * EDGE
    regs = span // SUB
    packs = rows // GROUPS
    vmem = pl.BlockSpec(memory_space=pltpu.VMEM)
    f32 = jnp.float32
    dma = pltpu.SemaphoreType.DMA
    slots = tiles * cap
    v, c = pl.pallas_call(
        functools.partial(main_kernel, tiles, bands, cap, total),
        out_shape=[
            jax.ShapeDtypeStruct((3, channels * rows, lanes), f32),
            jax.ShapeDtypeStruct((SUB, lanes), f32),
        ],
        in_specs=[vmem] * 5,
        out_specs=[vmem] * 2,
        scratch_shapes=[
            pltpu.VMEM((tiles, cap, width), f32),
            pltpu.VMEM((tiles, cap, width), f32),
            pltpu.VMEM((3, slots, (blocks + 1) * lanes), jnp.bfloat16),
            pltpu.VMEM((9, 3, rows, lanes), f32),
            pltpu.VMEM((3, 3, -(-(deep + 1) // SUB) * SUB, lanes), f32),
            pltpu.VMEM((5, deep, span, lanes), f32),
            pltpu.VMEM((blocks, deep, span, lanes), f32),
            pltpu.VMEM((blocks, regs, deep, SUB, lanes), f32),
            pltpu.VMEM((blocks, regs, deep, SUB, lanes), f32),
            pltpu.VMEM((2, regs, deep, SUB, lanes), f32),
            pltpu.VMEM((blocks, rows, span, lanes), f32),
            pltpu.VMEM((2, blocks, PASSES, wide, lanes), f32),
            pltpu.VMEM((2, blocks, PASSES, wide, lanes), f32),
            pltpu.VMEM((2, blocks, packs + 2, SUB, lanes), f32),
            pltpu.VMEM((2, blocks, packs + 2, SUB, lanes), f32),
            pltpu.VMEM((blocks, 2, packs, SUB, lanes), f32),
            pltpu.VMEM((STAGES, SUB, lanes), f32),
            pltpu.VMEM((SUB, lanes), f32),
            pltpu.VMEM((bands, SUB, lanes), f32),
            pltpu.VMEM((tiles, SUB, lanes), f32),
            dma((tiles - 1,)),
            dma((tiles - 1,)),
            dma((8,)),
            dma((8,)),
            dma,
            dma((2, blocks, 8)),
            dma((2, blocks, 8)),
            dma((tiles + bands - 2,)),
            dma((tiles + bands - 2,)),
        ],
        compiler_params=pltpu.CompilerParams(
            collective_id=1, has_side_effects=True, vmem_limit_bytes=48 * 1024 * 1024
        ),
        name="smooth_all",
    )(data, obs_tile.reshape(1, listed), obs_tile, maps, coef)

    v = v.reshape(3, channels, rows, lanes)
    block = wide
    out = pl.BlockSpec((block, rows, lanes), lambda i: (i, 0, 0))
    return pl.pallas_call(
        combine_kernel,
        grid=(blocks,),
        out_shape=[jax.ShapeDtypeStruct((total, rows, lanes), f32)] * 2,
        in_specs=[
            pl.BlockSpec((3, block, rows, lanes), lambda i: (0, i, 0, 0)),
            pl.BlockSpec((SUB, lanes), lambda i: (0, 0)),
        ],
        out_specs=[out, out],
        name="combine",
    )(v, c)


def solution(mesh):
    return jax.shard_map(
        local,
        mesh=mesh,
        in_specs=(
            P("lat", "lon"),
            P("lat", "lon"),
            P("lat", "lon"),
            P(),
            P(),
            P(("lon", "lat"), None),
            P(("lon", "lat")),
            P(("lon", "lat")),
            P(None, ("lon", "lat")),
        ),
        out_specs=(P(None, "lat", "lon"), P(None, "lat", "lon")),
        check_vma=False,
    )
```

time: 155 us -> 73.1 us (0.47)
  Pallas kernels: 145 us -> 63.4 us
    pallas_call x1, Pallas kernels: 140 us -> 58.2 us  [local(): pl.pallas_call(functools.partial(main_kernel, tiles, bands, cap, total),...]
where the time goes in v1:
time: 73.1 us; the launch traced here: 72.7 us
  Pallas kernels  63.4 us (87%)
  other arithmetic  4.53 us (6%)
  local copies, waits for them, and re-layouts  4.13 us (6%)
    pallas_call x1, Pallas kernels, local(): pl.pallas_call(functools.partial(main_kernel, tiles, bands, cap, total),...  58.2 us
    pallas_call x1, Pallas kernels, local(): pl.pallas_call(combine_kernel, grid=(blocks,), out_shape=[jax.ShapeDtypeS...  5.11 us
    unnamed x7, local copies, waits for them, and re-layouts  3.86 us

profile of v1, /device:TPU:0, one launch (start us, length us, event | category | flops | bytes accessed | tf_op | source)
XLA Modules:
  0.0 72.7 jit_solution(11158054496326519248)
XLA Ops:
  0.6 0.7 convert_element_type.26
  1.3 0.7 convert_element_type.25
  2.0 0.7 pad_multiply_fusion
  2.7 0.1 stack.26
  2.7 0.1 stack.27
  2.9 0.7 convert_bitcast_fusion
  3.6 0.7 pad_maximum_fusion.maps
  4.3 0.1 tile.12
  4.4 0.8 %copy.11.tile_col = s32[128,1]{1,0:T(8,128)S(1)} copy(s32[128,1]{0,1:T(1,128)} %param.14) | data formatting | bytes 1024 | tf_op args[5]
  5.2 1.1 %select_select_fusion.data = f32[256,128]{1,0:T(8,128)S(1)} fusion(f32[151,128]{1,0:T(8,128)} %param.17, f32[128]{0:T(128)S(1)} %convert_element_type.26, f32[128]{0:T(128)S(1)} %convert_element_type.25, pred[256]{0:T(512)(128)(4,1)S(1)} %get-tuple-element.8, pred[256]{0:T(512)(128)(4,1)S(1)} %get-tuple-element.9, pred[256]{0:T(512)(128)(4,1)S(1)} %iota_compare_fusion.2), kind=kLoop, calls=%fused_computation | loop fusion | flops 98304 | bytes 210176 | tf_op jit(solution)/shard_map/jit(_where)/select_n | solution.py:516
  6.2 0.0 copy-start.2
  6.2 0.6 copy-done.2
  6.9 58.2 %smooth_all.1 = (f32[3,2560,128]{2,1,0:T(8,128)S(1)}, f32[8,128]{1,0:T(8,128)S(1)}) custom-call(f32[256,128]{1,0:T(8,128)S(1)} %select_select_fusion.data, s32[1,128]{1,0:T(1,128)S(1)} %bitcast.12, s32[128,1]{1,0:T(8,128)S(1)} %copy.11.tile_col, f32[3,16,128]{2,1,0:T(8,128)S(1)} %pad_maximum_fusion.maps, f32[5,8,128]{2,1,0:T(8,128)S(1)} %pad.14.coef), custom_call_target="tpu_custom_call" | custom-call | tf_op jit(solution)/shard_map/smooth_all/pallas_call | solution.py:535
  65.1 0.0 copy-start
  65.1 1.9 %copy-done = f32[3,2560,128]{2,1,0:T(8,128)} copy-done((f32[3,2560,128]{2,1,0:T(8,128)}, f32[3,2560,128]{2,1,0:T(8,128)S(1)}, u32[]{:S(2)}) %copy-start) | copy-done | bytes 3932184
  67.0 0.0 copy-start.1
  67.0 0.6 copy-done.1
  67.6 5.1 %combine.1 = (f32[151,16,128]{2,1,0:T(8,128)}, f32[151,16,128]{2,1,0:T(8,128)}) custom-call(f32[3,160,16,128]{3,2,1,0:T(8,128)} %bitcast.11, f32[8,128]{1,0:T(8,128)} %copy-done.1), custom_call_target="tpu_custom_call" | custom-call | tf_op jit(solution)/shard_map/combine/pallas_call | solution.py:583
  (6 shorter events, 0.1 us)
Async XLA Ops:
  6.2 0.7 copy-start.2
  65.1 1.9 %copy-start = (f32[3,2560,128]{2,1,0:T(8,128)}, f32[3,2560,128]{2,1,0:T(8,128)S(1)}, u32[]{:S(2)}) copy-start(f32[3,2560,128]{2,1,0:T(8,128)S(1)} %get-tuple-element.4) | copy-start | bytes 11796484
  67.0 0.6 copy-start.1

commit v2 on v1

--- a/solution.py
+++ b/solution.py
@@ -42,13 +42,26 @@
     bands,
     cap,
     total,
-    data,
-    tile_row,
-    tile_col,
-    maps,
-    coef,
+    ke_in,
+    kn_in,
+    depth_in,
+    sigma_in,
+    precision_in,
+    tile_in,
+    col_in,
+    lat_in,
+    innovation_in,
     v_out,
     c_out,
+    depth_own,
+    sigma,
+    precision,
+    index,
+    innovation,
+    maps,
+    data,
+    rates,
+    coef,
     pay,
     rcv,
     values,
@@ -74,6 +87,7 @@
     map_send,
     map_recv,
     own_sem,
+    load_sem,
     halo_send,
     halo_recv,
     sum_send,
@@ -103,6 +117,25 @@
         else:
             pl.when(cond)(body)
 
+    loads = [
+        pltpu.make_async_copy(src, dst, load_sem.at[i])
+        for i, (src, dst) in enumerate(
+            (
+                (ke_in, maps.at[0]),
+                (kn_in, maps.at[1]),
+                (depth_in, depth_own),
+                (tile_in, index.at[0]),
+                (col_in, index.at[1]),
+                (lat_in, index.at[2]),
+                (innovation_in, innovation),
+                (sigma_in, sigma),
+                (precision_in, precision),
+            )
+        )
+    ]
+    for load in loads:
+        load.start()
+
     barrier = pltpu.get_barrier_semaphore()
 
     def greet(peer):
@@ -123,35 +156,46 @@
             device_id_type=MESH,
         )
 
-    listed = tile_row.shape[1]
+    def slot_of(dl, db):
+        return (dl + 1) * 3 + db + 1
+
+    def map_copy(d):
+        dl, db = ways[d]
+        return remote(
+            maps, near.at[slot_of(-dl, -db)], map_send.at[d], map_recv.at[d], at(dl, db)
+        )
+
+    for load in loads[:3]:
+        load.wait()
+    maps[2] = depth_own[...].astype(jnp.float32)
+    diagonal = jnp.where(has_s, 2, 0) + jnp.where(has_n, 2, 0)
+    pl.semaphore_wait(barrier, len(beside) + len(along) + diagonal)
+    for d in (4, 5, 6, 7, 2, 3, 0, 1):
+        only(there[ways[d][1]], lambda d=d: map_copy(d).start())
+
+    for load in loads[3:7]:
+        load.wait()
+    listed = index.shape[2]
     slots = tiles * cap
-    same = tile_col[...] == tile_row[...]
+    width = data.shape[0]
+    kinds_at = -(-total // SUB) * SUB
+    data[kinds_at - SUB :] = jnp.zeros((width - kinds_at + SUB, listed), jnp.float32)
+    data[0:total] = innovation[...]
+    data[kinds_at : kinds_at + 1] = jnp.ones((1, listed), jnp.float32)
+    data[kinds_at + 1 : kinds_at + 2] = index[1].astype(jnp.float32)
+    data[kinds_at + 2 : kinds_at + 3] = index[2].astype(jnp.float32)
+    tile_row = jnp.broadcast_to(index[0].astype(jnp.float32), (listed, listed))
     earlier = iota((listed, listed), 0) < iota((listed, listed), 1)
-    rank = jnp.sum(jnp.where(same & earlier, 1.0, 0.0), 0, keepdims=True)
-    slot = tile_row[...] * cap + rank.astype(jnp.int32)
+    same = (tile_row == tile_row.T) & earlier
+    rank = jnp.sum(jnp.where(same, 1.0, 0.0), 0, keepdims=True)
+    slot = index[0] * cap + rank.astype(jnp.int32)
     chosen = ones_where(iota((slots, listed), 0) == slot)
-    width = data.shape[0]
     packed = jnp.zeros((slots, width), jnp.float32)
     for part in split3(data[...]):
         packed = packed + lax.dot_general(
             chosen, part, (((1,), (1,)), ((), ())), preferred_element_type=jnp.float32
         )
     pay[...] = packed.reshape(tiles, cap, width)
-
-    diagonal = jnp.where(has_s, 2, 0) + jnp.where(has_n, 2, 0)
-    pl.semaphore_wait(barrier, len(beside) + len(along) + diagonal)
-
-    def slot_of(dl, db):
-        return (dl + 1) * 3 + db + 1
-
-    def map_copy(d):
-        dl, db = ways[d]
-        return remote(
-            maps, near.at[slot_of(-dl, -db)], map_send.at[d], map_recv.at[d], at(dl, db)
-        )
-
-    for d in (4, 5, 6, 7, 2, 3, 0, 1):
-        only(there[ways[d][1]], lambda d=d: map_copy(d).start())
     obs = []
     for k, peer in enumerate(along):
         copy = remote(pay.at[peer[0]], rcv.at[lon], obs_send.at[k], obs_recv.at[k], peer)
@@ -193,6 +237,27 @@
         return carry
 
     lax.fori_loop(0, blocks, clear, 0)
+
+    for load in loads[7:]:
+        load.wait()
+    levels = (total - 1) // 2
+    rates[...] = jnp.zeros(rates.shape, jnp.float32)
+    rates[0:1, 0:total] = sigma[...] * precision[...]
+    rates[1:2, 0:total] = sigma[...] * sigma[...] * precision[...]
+    coef_lane = iota((SUB, lanes), 1)
+    for b in range(blocks):
+        tile, first = b * wide // lanes, b * wide % lanes
+        piece = rates[:, tile * lanes : tile * lanes + lanes]
+        out = None
+        for g in range(GROUPS):
+            move = (wide * g - first) % lanes
+            moved = pltpu.roll(piece, move, 1) if move else piece
+            out = moved if g == 0 else jnp.where(coef_lane >= wide * g, moved, out)
+        coef[b, 1:3] = out[0:2]
+        channel = coef_lane[0:1] % wide + b * wide
+        level = jnp.where(channel < 2 * levels, channel % levels, 0)
+        level = jnp.where(channel < total, level, 2 * levels)
+        coef[b, 0:1] = level.astype(jnp.float32)
 
     for d in range(8):
         dl, db = ways[d]
@@ -256,17 +321,17 @@
     for copy in obs:
         copy.wait()
     arrived = rcv[...].reshape(slots, width)
-    columns = arrived[:, total + 1 : total + 2]
+    columns = arrived[:, kinds_at + 1 : kinds_at + 2]
     flat = (blocks + 1) * lanes
     source, goal = iota((width, flat), 0), iota((width, flat), 1)
-    channel = jnp.where(goal < blocks * lanes, goal // lanes * wide + goal % wide, total)
+    channel = jnp.where(goal < blocks * lanes, goal // lanes * wide + goal % wide, kinds_at)
     to_flat = ones_where(source == channel)
     group = (iota((slots, flat), 1) % lanes // wide * wide).astype(jnp.float32)
     mine = (columns >= group) & (columns < group + wide)
     for i, part in enumerate(split3(arrived)):
         wide_part = jnp.dot(part, to_flat, preferred_element_type=jnp.float32)
         values[i] = jnp.where(mine, wide_part, 0.0).astype(jnp.bfloat16)
-    picker = ones_where(iota((SUB, width), 1) == iota((SUB, width), 0) + total + 1)
+    picker = ones_where(iota((SUB, width), 1) == iota((SUB, width), 0) + kinds_at + 1)
     turned = lax.dot_general(
         picker,
         arrived.astype(jnp.bfloat16),
@@ -423,16 +488,23 @@
                 for a in range(packs):
                     first = PASSES + GROUPS * a
                     square = f[b, first : first + GROUPS, own_cols].reshape(lanes, lanes).T
+                    pieces = [square[wide * g : wide * g + wide] for g in range(GROUPS)]
+                    lane_all = iota((wide, lanes), 1)
+                    step = GROUPS // 2
+                    while step:
+                        move = step * wide
+                        low = lane_all // move % 2 == 0
+                        for g in range(GROUPS):
+                            if g // step % 2 == 0:
+                                one, two = pieces[g], pieces[g + step]
+                                pieces[g] = jnp.where(low, one, pltpu.roll(two, move, 1))
+                                pieces[g + step] = jnp.where(
+                                    low, pltpu.roll(one, lanes - move, 1), two
+                                )
+                        step //= 2
                     for i in range(GROUPS):
-                        out = None
-                        for g in range(GROUPS):
-                            piece = square[wide * g : wide * g + wide]
-                            move = wide * (g - i) % lanes
-                            piece = pltpu.roll(piece, move, 1) if move else piece
-                            lane_all = iota((wide, lanes), 1)
-                            out = piece if g == 0 else jnp.where(lane_all >= wide * g, piece, out)
                         begin = b * (wide * rows) + GROUPS * a + i
-                        v_out[lax.div(e, 2), pl.ds(begin, wide, stride=rows), :] = out
+                        v_out[lax.div(e, 2), pl.ds(begin, wide, stride=rows), :] = pieces[i]
 
             @pl.when((e == STAGES - 1) & (b == blocks // 2))
             def _():
@@ -480,14 +552,21 @@
         c_out[i : i + 1, :] = jnp.broadcast_to(value, (1, lanes))
 
 
-def combine_kernel(v, c, increment, residual):
-    shape = increment.shape
-
-    def scalar(i):
-        return jnp.broadcast_to(c[i : i + 1, :].reshape(1, 1, shape[2]), shape)
-
-    increment[...] = scalar(0) * v[0] + scalar(1) * v[1]
-    residual[...] = scalar(2) * v[0] + scalar(3) * v[1] + scalar(4) * v[2]
+def combine_kernel(block, v, c, increment, residual, held, sems):
+    size, lanes = increment.shape
+    copies = []
+    for n, first in enumerate(range(0, size, block)):
+        count = min(block, size - first)
+        part = pl.ds(first, count)
+        zero, one, two = v[0, part], v[1, part], v[2, part]
+        held[0, part] = c[0:1] * zero + c[1:2] * one
+        held[1, part] = c[2:3] * zero + c[3:4] * one + c[4:5] * two
+        for i, target in enumerate((increment, residual)):
+            copy = pltpu.make_async_copy(held.at[i, part], target.at[part], sems.at[i, n])
+            copy.start()
+            copies.append(copy)
+    for copy in copies:
+        copy.wait()
 
 
 def local(
@@ -501,28 +580,7 @@
     wide = lanes // GROUPS
     blocks = -(-total // wide)
     channels = blocks * wide
-    levels = (total - 1) // 2
-    width = -(-(total + 3) // 128) * 128
-
-    data = jnp.concatenate(
-        [
-            innovation,
-            jnp.zeros((width - total, listed), jnp.float32),
-        ]
-    )
-    row = lax.broadcasted_iota(jnp.int32, (width, listed), 0)
-    data = jnp.where(row == total, 1.0, data)
-    data = jnp.where(row == total + 1, obs_col.astype(jnp.float32)[None], data)
-    data = jnp.where(row == total + 2, obs_lat.astype(jnp.float32)[None], data)
-    maps = jnp.stack([kappa_east, kappa_north, depth.astype(jnp.float32)])
-    ids = jnp.arange(channels, dtype=jnp.int32)
-    level = jnp.where(ids < 2 * levels, ids % levels, 0)
-    level = jnp.where(ids < total, level, 2 * levels).astype(jnp.float32)
-    scale = jnp.pad(sigma, (0, channels - total))
-    weight = jnp.pad(obs_precision, (0, channels - total))
-    coef = jnp.stack([level, scale * weight, scale * scale * weight])
-    coef = jnp.tile(coef.reshape(3, blocks, wide), (1, 1, GROUPS)).transpose(1, 0, 2)
-    coef = jnp.pad(coef, ((0, 0), (0, SUB - 3), (0, 0)))
+    width = -(-(-(-total // SUB) * SUB + SUB) // 128) * 128
 
     deep = rows + 2 * PASSES
     span = wide + 2 * EDGE
@@ -538,9 +596,18 @@
             jax.ShapeDtypeStruct((3, channels * rows, lanes), f32),
             jax.ShapeDtypeStruct((SUB, lanes), f32),
         ],
-        in_specs=[vmem] * 5,
+        in_specs=[pl.BlockSpec(memory_space=pltpu.HBM)] * 9,
         out_specs=[vmem] * 2,
         scratch_shapes=[
+            pltpu.VMEM((rows, lanes), jnp.int32),
+            pltpu.VMEM((1, total), f32),
+            pltpu.VMEM((1, total), f32),
+            pltpu.VMEM((3, 1, listed), jnp.int32),
+            pltpu.VMEM((total, listed), f32),
+            pltpu.VMEM((3, rows, lanes), f32),
+            pltpu.VMEM((width, listed), f32),
+            pltpu.VMEM((SUB, -(-channels // lanes) * lanes), f32),
+            pltpu.VMEM((blocks, SUB, lanes), f32),
             pltpu.VMEM((tiles, cap, width), f32),
             pltpu.VMEM((tiles, cap, width), f32),
             pltpu.VMEM((3, slots, (blocks + 1) * lanes), jnp.bfloat16),
@@ -566,6 +633,7 @@
             dma((8,)),
             dma((8,)),
             dma,
+            dma((9,)),
             dma((2, blocks, 8)),
             dma((2, blocks, 8)),
             dma((tiles + bands - 2,)),
@@ -575,22 +643,35 @@
             collective_id=1, has_side_effects=True, vmem_limit_bytes=48 * 1024 * 1024
         ),
         name="smooth_all",
-    )(data, obs_tile.reshape(1, listed), obs_tile, maps, coef)
-
-    v = v.reshape(3, channels, rows, lanes)
-    block = wide
-    out = pl.BlockSpec((block, rows, lanes), lambda i: (i, 0, 0))
-    return pl.pallas_call(
-        combine_kernel,
-        grid=(blocks,),
-        out_shape=[jax.ShapeDtypeStruct((total, rows, lanes), f32)] * 2,
-        in_specs=[
-            pl.BlockSpec((3, block, rows, lanes), lambda i: (0, i, 0, 0)),
-            pl.BlockSpec((SUB, lanes), lambda i: (0, 0)),
-        ],
-        out_specs=[out, out],
+    )(
+        *[
+            pltpu.with_memory_space_constraint(x, pltpu.HBM)
+            for x in (
+                kappa_east,
+                kappa_north,
+                depth,
+                sigma.reshape(1, total),
+                obs_precision.reshape(1, total),
+                obs_tile.reshape(1, listed),
+                obs_col.reshape(1, listed),
+                obs_lat.reshape(1, listed),
+                innovation,
+            )
+        ]
+    )
+
+    block = wide * rows
+    increment, residual = pl.pallas_call(
+        functools.partial(combine_kernel, block),
+        out_shape=[jax.ShapeDtypeStruct((total * rows, lanes), f32)] * 2,
+        in_specs=[vmem] * 2,
+        out_specs=[pl.BlockSpec(memory_space=pl.ANY)] * 2,
+        scratch_shapes=[pltpu.VMEM((2, total * rows, lanes), f32), dma((2, blocks))],
+        compiler_params=pltpu.CompilerParams(vmem_limit_bytes=10 * 1024 * 1024),
         name="combine",
     )(v, c)
+    shape = (total, rows, lanes)
+    return increment.reshape(shape), residual.reshape(shape)
 
 
 def solution(mesh):

time: 73.1 us -> 60.2 us (0.82)
  other arithmetic: 4.53 us -> 0 us
  local copies, waits for them, and re-layouts: 4.13 us -> 0 us
  Pallas kernels: 63.4 us -> 59.4 us
    unnamed x7 -> x0, local copies, waits for them, and re-layouts: 3.86 us -> none
    pallas_call x1, Pallas kernels: 5.11 us -> 1.6 us  [local(): pl.pallas_call(functools.partial(combine_kernel, block), out_shape=[jax.S...]
    another operation x3 -> x0, other arithmetic: 1.43 us -> none  [the longest x2 1.42 us: local(): maps = jnp.stack([kappa_east, kappa_north, depth.astype(jnp.float32)])]
    convert_element_type x3 -> x0, other arithmetic: 1.33 us -> none  [the longest x1 0.66 us: local(): data = jnp.where(row == total + 1, obs_col.astype(jnp.float32)[None], data)]
    select_n x1 -> x0, other arithmetic: 1.05 us -> none  [local(): data = jnp.where(row == total + 2, obs_lat.astype(jnp.float32)[None], data)]
where the time goes in v2:
time: 60.2 us; the launch traced here: 60 us
  Pallas kernels  59.4 us (99%)
  between operations  0.64 us (1%)
    pallas_call x1, Pallas kernels, local(): pl.pallas_call(functools.partial(main_kernel, tiles, bands, cap, total),...  57.8 us
    pallas_call x1, Pallas kernels, local(): pl.pallas_call(functools.partial(combine_kernel, block), out_shape=[jax.S...  1.6 us

profile of v2, /device:TPU:0, one launch (start us, length us, event | category | flops | bytes accessed | tf_op | source)
XLA Modules:
  0.0 60.0 jit_solution(1387081199002941845)
XLA Ops:
  0.6 57.8 %smooth_all.1 = (f32[3,2560,128]{2,1,0:T(8,128)S(1)}, f32[8,128]{1,0:T(8,128)S(1)}) custom-call(f32[16,128]{1,0:T(8,128)} %ke_in.1, f32[16,128]{1,0:T(8,128)} %kn_in.1, s32[16,128]{1,0:T(8,128)} %depth_in.1, f32[1,151]{1,0:T(1,128)} %bitcast.7, f32[1,151]{1,0:T(1,128)} %bitcast.8, s32[1,128]{1,0:T(1,128)} %bitcast.9, s32[1,128]{1,0:T(1,128)} %bitcast.10, ...), custom_call_target="tpu_custom_call" | custom-call | tf_op jit(solution)/shard_map/smooth_all/pallas_call | solution.py:593
  58.4 1.6 %combine.1 = (f32[2416,128]{1,0:T(8,128)}, f32[2416,128]{1,0:T(8,128)}) custom-call(f32[3,2560,128]{2,1,0:T(8,128)S(1)} %get-tuple-element.6.v, f32[8,128]{1,0:T(8,128)S(1)} %get-tuple-element.7.c), custom_call_target="tpu_custom_call" | custom-call | tf_op jit(solution)/shard_map/combine/pallas_call | solution.py:664

commit v3 on v2

v3 whole, which is shorter than its diff:
```python
import functools

import jax
import jax.numpy as jnp
from jax import lax
from jax.experimental import pallas as pl
from jax.experimental.pallas import tpu as pltpu
from jax.sharding import PartitionSpec as P

MESH = pl.DeviceIdType.MESH
SUB = 8
PASSES = 5
STAGES = 5
EDGE = 8


SCRATCH = ("base", "values", "coef", "f", "fe", "fn", "tmp", "gain")
SCRATCH += ("hs", "hn", "pw", "pe", "pk", "send", "recv")


class Layout:
    def __init__(self, first, blocks, groups, rows, lanes):
        self.first, self.blocks, self.groups = first, blocks, groups
        self.wide = lanes // groups
        self.span = self.wide + 2 * EDGE
        self.regs = self.span // SUB
        self.packs = rows // groups
        self.corner = (PASSES - 1) // groups
        self.rows, self.lanes = rows, lanes

    def bind(self, refs):
        for name, ref in zip(SCRATCH, refs):
            setattr(self, name, ref)

    def shapes(self, slots):
        f32, dma = jnp.float32, pltpu.SemaphoreType.DMA
        rows, lanes, blocks = self.rows, self.lanes, self.blocks
        deep = rows + 2 * PASSES
        faces = pltpu.VMEM((blocks, self.regs, deep, SUB, lanes), f32)
        beside = pltpu.VMEM((2, blocks, PASSES, self.wide, lanes), f32)
        edge = pltpu.VMEM((2, blocks, self.packs + 2 * self.corner, SUB, lanes), f32)
        return [
            pltpu.VMEM((5, deep, self.span, lanes), f32),
            pltpu.VMEM((3, slots, (blocks + 1) * lanes), jnp.bfloat16),
            pltpu.VMEM((blocks, SUB, lanes), f32),
            pltpu.VMEM((blocks, deep, self.span, lanes), f32),
            faces,
            faces,
            pltpu.VMEM((2, self.regs, deep, SUB, lanes), f32),
            pltpu.VMEM((blocks, rows, self.span, lanes), f32),
            beside,
            beside,
            edge,
            edge,
            pltpu.VMEM((blocks, 2, self.packs, SUB, lanes), f32),
            dma((2, blocks, 8)),
            dma((2, blocks, 8)),
        ]


def layouts_of(total, rows, lanes):
    pairs = total // (lanes // 2)
    left = total - pairs * (lanes // 2)
    out = [Layout(0, pairs, 2, rows, lanes)]
    if left:
        out.append(Layout(pairs * (lanes // 2), -(-left // (lanes // 4)), 4, rows, lanes))
    return out


def split3(x):
    high = x.astype(jnp.bfloat16)
    left = x - high.astype(jnp.float32)
    middle = left.astype(jnp.bfloat16)
    low = (left - middle.astype(jnp.float32)).astype(jnp.bfloat16)
    return high, middle, low


def chunks(first, end, most=8):
    count = -(-(end - first) // most)
    cuts = [first + (end - first) * i // count for i in range(count + 1)]
    return list(zip(cuts[:-1], cuts[1:]))


def iota(shape, dim):
    return lax.broadcasted_iota(jnp.int32, shape, dim)


def ones_where(mask):
    return jnp.where(mask, 1.0, 0.0).astype(jnp.bfloat16)


def main_kernel(
    tiles,
    bands,
    cap,
    total,
    ke_in,
    kn_in,
    depth_in,
    sigma_in,
    precision_in,
    tile_in,
    col_in,
    lat_in,
    innovation_in,
    v_out,
    c_out,
    depth_own,
    sigma,
    precision,
    index,
    innovation,
    maps,
    data,
    rates,
    pay,
    rcv,
    near,
    ext,
    mom,
    red,
    red_all,
    obs_send,
    obs_recv,
    map_send,
    map_recv,
    own_sem,
    load_sem,
    sum_send,
    sum_recv,
    *rest,
):
    lon, lat = lax.axis_index("lon"), lax.axis_index("lat")
    rows, lanes = maps.shape[1], maps.shape[2]
    deep = rows + 2 * PASSES
    last = rows + PASSES
    layouts = layouts_of(total, rows, lanes)
    for n, lay in enumerate(layouts):
        lay.bind(rest[n * len(SCRATCH) : (n + 1) * len(SCRATCH)])
    has_s, has_n = lat > 0, lat < bands - 1

    def at(dl, db):
        return lax.rem(lon + dl + tiles, tiles), lax.rem(lat + db + bands, bands)

    along = [(lax.rem(lon + k, tiles), lat) for k in range(1, tiles)]
    ways = [(0, -1), (0, 1), (-1, 0), (1, 0), (-1, -1), (1, -1), (-1, 1), (1, 1)]
    there = {-1: has_s, 0: None, 1: has_n}

    def only(cond, body):
        if cond is None:
            body()
        else:
            pl.when(cond)(body)

    loads = [
        pltpu.make_async_copy(src, dst, load_sem.at[i])
        for i, (src, dst) in enumerate(
            (
                (ke_in, maps.at[0]),
                (kn_in, maps.at[1]),
                (depth_in, depth_own),
                (tile_in, index.at[0]),
                (col_in, index.at[1]),
                (lat_in, index.at[2]),
                (innovation_in, innovation),
                (sigma_in, sigma),
                (precision_in, precision),
            )
        )
    ]
    for load in loads:
        load.start()

    barrier = pltpu.get_barrier_semaphore()

    def greet(peer):
        pl.semaphore_signal(barrier, inc=1, device_id=peer, device_id_type=MESH)

    def greet_all(k, carry):
        peer = lax.rem(lon * bands + lat + k, tiles * bands)
        greet((lax.div(peer, bands), lax.rem(peer, bands)))
        return carry

    lax.fori_loop(1, tiles * bands, greet_all, 0)

    def remote(src, dst, send, recv, peer):
        return pltpu.make_async_remote_copy(
            src_ref=src,
            dst_ref=dst,
            send_sem=send,
            recv_sem=recv,
            device_id=peer,
            device_id_type=MESH,
        )

    def slot_of(dl, db):
        return (dl + 1) * 3 + db + 1

    def map_copy(d):
        dl, db = ways[d]
        return remote(
            maps, near.at[slot_of(-dl, -db)], map_send.at[d], map_recv.at[d], at(dl, db)
        )

    for load in loads[:3]:
        load.wait()
    maps[2] = depth_own[...].astype(jnp.float32)
    for load in loads[3:7]:
        load.wait()
    listed = index.shape[2]
    slots = tiles * cap
    width = data.shape[0]
    kinds_at = -(-total // SUB) * SUB
    data[kinds_at - SUB :] = jnp.zeros((width - kinds_at + SUB, listed), jnp.float32)
    data[0:total] = innovation[...]
    data[kinds_at : kinds_at + 1] = jnp.ones((1, listed), jnp.float32)
    data[kinds_at + 1 : kinds_at + 2] = index[1].astype(jnp.float32)
    data[kinds_at + 2 : kinds_at + 3] = index[2].astype(jnp.float32)
    tile_row = jnp.broadcast_to(index[0].astype(jnp.float32), (listed, listed))
    earlier = iota((listed, listed), 0) < iota((listed, listed), 1)
    same = (tile_row == tile_row.T) & earlier
    rank = jnp.sum(jnp.where(same, 1.0, 0.0), 0, keepdims=True)
    slot = index[0] * cap + rank.astype(jnp.int32)
    chosen = ones_where(iota((slots, listed), 0) == slot)
    packed = jnp.zeros((slots, width), jnp.float32)
    for part in split3(data[...]):
        packed = packed + lax.dot_general(
            chosen, part, (((1,), (1,)), ((), ())), preferred_element_type=jnp.float32
        )
    share = lanes * SUB // cap
    packed = packed.reshape(tiles, cap, width)
    pay[:, 0:cap] = packed[:, :, 0:lanes]
    low = iota((SUB, lanes), 1)
    for n in range(tiles):
        out = packed[n, 0:SUB, lanes:]
        for i in range(1, cap // SUB):
            piece = pltpu.roll(packed[n, SUB * i : SUB * i + SUB, lanes:], share * i, 1)
            out = jnp.where(low >= share * i, piece, out)
        pay[n, cap:] = out
    pl.semaphore_wait(barrier, tiles * bands - 1)
    obs = []
    for k, peer in enumerate(along):
        copy = remote(pay.at[peer[0]], rcv.at[lon], obs_send.at[k], obs_recv.at[k], peer)
        copy.start()
        obs.append(copy)
    for d in (4, 5, 6, 7, 2, 3, 0, 1):
        only(there[ways[d][1]], lambda d=d: map_copy(d).start())
    own = pltpu.make_async_copy(pay.at[lon], rcv.at[lon], own_sem)
    own.start()

    nothing = jnp.zeros(maps.shape, jnp.float32)
    near[slot_of(0, 0)] = maps[...]

    @pl.when(jnp.logical_not(has_s))
    def _():
        for dl in (-1, 0, 1):
            near[slot_of(dl, -1)] = nothing
        for lay in layouts:
            lay.hs[...] = jnp.zeros(lay.hs.shape, jnp.float32)
            for ref in (lay.pw, lay.pe):
                none = jnp.zeros(ref.shape[:2] + (lay.corner,) + ref.shape[3:], jnp.float32)
                ref[:, :, 0 : lay.corner] = none

    @pl.when(jnp.logical_not(has_n))
    def _():
        for dl in (-1, 0, 1):
            near[slot_of(dl, 1)] = nothing
        for lay in layouts:
            lay.hn[...] = jnp.zeros(lay.hn.shape, jnp.float32)
            for ref in (lay.pw, lay.pe):
                none = jnp.zeros(ref.shape[:2] + (lay.corner,) + ref.shape[3:], jnp.float32)
                ref[:, :, lay.packs + lay.corner :] = none

    mom[...] = jnp.zeros(mom.shape, jnp.float32)
    red[...] = jnp.zeros(red.shape, jnp.float32)
    ext[...] = jnp.zeros(ext.shape, jnp.float32)

    for lay in layouts:
        for b in range(lay.blocks):
            for r in (0, deep - 1):
                lay.f[b, r] = jnp.zeros((lay.span, lanes), jnp.float32)
            for c in (0, lay.span - EDGE):
                lay.f[b, :, c : c + EDGE] = jnp.zeros((deep, EDGE, lanes), jnp.float32)
                lay.gain[b, :, c : c + EDGE] = jnp.zeros((rows, EDGE, lanes), jnp.float32)

    for load in loads[7:]:
        load.wait()
    levels = (total - 1) // 2
    rates[...] = jnp.zeros(rates.shape, jnp.float32)
    rates[0:1, 0:total] = sigma[...] * precision[...]
    rates[1:2, 0:total] = sigma[...] * sigma[...] * precision[...]
    coef_lane = iota((SUB, lanes), 1)
    for lay in layouts:
        for b in range(lay.blocks):
            start = lay.first + b * lay.wide
            tile, first = start // lanes, start % lanes
            piece = rates[:, tile * lanes : tile * lanes + lanes]
            out = None
            for g in range(lay.groups):
                move = (lay.wide * g - first) % lanes
                moved = pltpu.roll(piece, move, 1) if move else piece
                out = moved if g == 0 else jnp.where(coef_lane >= lay.wide * g, moved, out)
            lay.coef[b, 1:3] = out[0:2]
            channel = coef_lane[0:1] % lay.wide + start
            level = jnp.where(channel < 2 * levels, channel % levels, 0)
            level = jnp.where(channel < total, level, 2 * levels)
            lay.coef[b, 0:1] = level.astype(jnp.float32)

    own_mask = iota((1, SUB, lanes), 2) % SUB == iota((1, SUB, lanes), 1)
    picked = jnp.where(own_mask, maps[2][:, None, :], 0.0)
    picked = picked.reshape(rows * SUB, lanes).astype(jnp.bfloat16)
    for lay in layouts:
        tiles_of = lay.wide // SUB
        column = iota((lanes, tiles_of * lanes), 0)
        target = iota((lanes, tiles_of * lanes), 1)
        start = target % lanes // lay.wide * lay.wide + target // lanes * SUB
        to_lane = ones_where((column >= start) & (column < start + SUB))
        out = jnp.dot(picked, to_lane, preferred_element_type=jnp.float32)
        for i in range(tiles_of):
            piece = out[:, lanes * i : lanes * i + lanes].reshape(rows, SUB, lanes)
            lay.base[4, PASSES:last, EDGE + SUB * i : EDGE + SUB * i + SUB] = piece

    own.wait()
    for copy in obs:
        copy.wait()
    first_half = rcv[:, 0:cap].reshape(slots, lanes)
    second = []
    for n in range(tiles):
        for i in range(cap // SUB):
            piece = rcv[n, cap:]
            second.append(pltpu.roll(piece, lanes - share * i, 1) if i else piece)
    arrived = jnp.concatenate([first_half, jnp.concatenate(second, 0)], 1)
    arrived = jnp.where(iota((slots, width), 1) < lanes + share, arrived, 0.0)
    columns = arrived[:, kinds_at + 1 : kinds_at + 2]
    picker = ones_where(iota((SUB, width), 1) == iota((SUB, width), 0) + kinds_at + 1)
    turned = lax.dot_general(
        picker,
        arrived.astype(jnp.bfloat16),
        (((1,), (1,)), ((), ())),
        preferred_element_type=jnp.float32,
    )
    pieces = split3(arrived)
    for lay in layouts:
        wide, blocks = lay.wide, lay.blocks
        flat = (blocks + 1) * lanes
        source, goal = iota((width, flat), 0), iota((width, flat), 1)
        channel = goal // lanes * wide + goal % wide + lay.first
        to_flat = ones_where(source == jnp.where(goal < blocks * lanes, channel, kinds_at))
        group = (iota((slots, flat), 1) % lanes // wide * wide).astype(jnp.float32)
        mine = (columns >= group) & (columns < group + wide)
        for i, piece in enumerate(pieces):
            wide_part = jnp.dot(piece, to_flat, preferred_element_type=jnp.float32)
            lay.values[i] = jnp.where(mine, wide_part, 0.0).astype(jnp.bfloat16)
        place = turned[1:2] * wide + turned[0:1] - jnp.floor(turned[0:1] / wide) * wide
        spots = iota((rows * wide, slots), 0).astype(jnp.float32)
        to_cell = ones_where(spots == place)
        own_cols = slice(EDGE, EDGE + wide)
        depths = lay.base[4, PASSES:last, own_cols]

        def cells_of(b, count):
            out = jnp.zeros((rows * wide, lanes), jnp.float32)
            for i in range(count):
                out = out + jnp.dot(
                    to_cell,
                    lay.values[i, :, b * lanes : (b + 1) * lanes],
                    preferred_element_type=jnp.float32,
                )
            return out.reshape(rows, wide, lanes)

        counts = cells_of(blocks, 1)
        for b in range(blocks):
            wet = depths > lay.coef[b, 0:1][None]
            cells = lay.coef[b, 1:2][None] * cells_of(b, 3)
            lay.f[b, PASSES:last, own_cols] = jnp.where(wet, cells, 0.0)
            lay.gain[b, :, own_cols] = jnp.where(wet, lay.coef[b, 2:3][None] * counts, 0.0)

    lane = iota((SUB, lanes), 1)
    subs = iota((SUB, lanes), 0)

    def halo(lay, par, b, d):
        dl, db = ways[d]
        send, recv = lay.send.at[par, b, d], lay.recv.at[par, b, d]
        if dl == 0:
            first = PASSES if db < 0 else last - PASSES
            src = lay.f.at[b, pl.ds(first, PASSES), pl.ds(EDGE, lay.wide)]
            dst = (lay.hn if db < 0 else lay.hs).at[par, b]
        else:
            pack, to = (0, lay.pe) if dl < 0 else (1, lay.pw)
            packs, corner = lay.packs, lay.corner
            if db == 0:
                src = lay.pk.at[b, pack]
                dst = to.at[par, b, pl.ds(corner, packs)]
            else:
                src = lay.pk.at[b, pack, pl.ds(0 if db < 0 else packs - corner, corner)]
                dst = to.at[par, b, pl.ds(packs + corner if db < 0 else 0, corner)]
        return remote(src, dst, send, recv, at(dl, db))

    def emit(lay, par, b):
        wide, groups = lay.wide, lay.groups
        for a in range(lay.packs):
            for side, first, from_lane in ((0, EDGE, 0), (1, wide, lanes - wide)):
                out = None
                for i in range(groups):
                    piece = lay.f[b, PASSES + groups * a + i, first : first + EDGE]
                    move = (wide * i - from_lane) % lanes
                    piece = pltpu.roll(piece, move, 1) if move else piece
                    out = piece if out is None else jnp.where(lane >= wide * i, piece, out)
                lay.pk[b, side, a] = out
        for d in (2, 3, 4, 5, 6, 7, 0, 1):
            only(there[ways[d][1]], lambda d=d: halo(lay, par, b, d).start())

    for lay in layouts:
        for b in range(lay.blocks):
            emit(lay, 0, b)

    for d in range(8):
        dl, db = ways[d]
        only(there[-db], lambda d=d: map_copy(d).wait_recv())
    for d in range(8):
        only(there[ways[d][1]], lambda d=d: map_copy(d).wait_send())

    for m in range(3):
        for side in range(3):
            ext[m, side, 0:PASSES] = near[3 * side, m, rows - PASSES : rows]
            ext[m, side, PASSES:last] = near[3 * side + 1, m]
            ext[m, side, last:deep] = near[3 * side + 2, m, 0:PASSES]
    edge = iota((deep, lanes), 1) == lanes - 1
    east, north, depth = [], [], [ext[2, side, 0:deep] for side in range(3)]
    ahead = [pltpu.roll(ext[2, side], lanes - 1, 1)[0:deep] for side in range(3)]
    for side in range(3):
        moved = ahead[side]
        if side < 2:
            moved = jnp.where(edge, ahead[side + 1], moved)
        east.append(jnp.minimum(depth[side], moved))
        north.append(jnp.minimum(depth[side], ext[2, side, 1 : deep + 1]))
    reach = 3 * lanes
    for lay in layouts:
        column = iota((reach, lay.regs * lanes), 0) - lanes + EDGE
        target = iota((reach, lay.regs * lanes), 1)
        start = target % lanes // lay.wide * lay.wide + target // lanes * SUB
        lay.to_lane = ones_where((column >= start) & (column < start + SUB))
    sub_mask = iota((1, SUB, reach), 2) % SUB == iota((1, SUB, reach), 1)
    kinds = (
        [ext[0, side, 0:deep] for side in range(3)],
        east,
        [ext[1, side, 0:deep] for side in range(3)],
        north,
    )
    for m, kind in enumerate(kinds):
        line = jnp.concatenate(kind, 1)
        parts = [line] if m in (1, 3) else [x.astype(jnp.float32) for x in split3(line)]
        picked = [
            jnp.where(sub_mask, part[:, None, :], 0.0)
            .reshape(deep * SUB, reach)
            .astype(jnp.bfloat16)
            for part in parts
        ]
        for lay in layouts:
            out = jnp.zeros((deep * SUB, lay.regs * lanes), jnp.float32)
            for part in picked:
                out = out + jnp.dot(part, lay.to_lane, preferred_element_type=jnp.float32)
            for i in range(lay.regs):
                piece = out[:, lanes * i : lanes * i + lanes].reshape(deep, SUB, lanes)
                lay.base[m, :, SUB * i : SUB * i + SUB] = piece

    def build(lay, b, carry):
        level = lay.coef[b, 0:1]
        base, regs = lay.base, lay.regs
        for j in range(regs):
            pick = pl.ds(j, SUB, stride=regs)
            for r in range(deep):
                east_wet = base[1, r, pick, :] > level
                north_wet = base[3, r, pick, :] > level
                lay.fe[b, j, r] = jnp.where(east_wet, base[0, r, pick, :], 0.0)
                lay.fn[b, j, r] = jnp.where(north_wet, base[2, r, pick, :], 0.0)
        return carry

    for lay in layouts:
        lax.fori_loop(0, lay.blocks, functools.partial(build, lay), 0)

    everyone = tiles * bands
    me = lon * bands + lat

    def sum_copy(k):
        peer = lax.rem(me + k, everyone)
        return remote(
            red, red_all.at[k - 1], sum_send, sum_recv, (lax.div(peer, bands), lax.rem(peer, bands))
        )

    def one_pass(lay, b, t, finish):
        f, fe, fn, tmp, regs = lay.f, lay.fe, lay.fn, lay.tmp, lay.regs

        def old(j, lo, hi):
            if t == 0:
                return jnp.stack(
                    [f[b, r, pl.ds(j, SUB, stride=regs), :] for r in range(lo, hi)]
                )
            return tmp[(t + 1) % 2, j, lo:hi]

        for lo, hi in chunks(t + 1, deep - 1 - t):
            v = old(0, lo - 1, hi + 1)
            wrap = pltpu.roll(v[1:-1], SUB - 1, 1)
            end = old(regs - 1, lo, hi)
            end = fe[b, regs - 1, lo:hi] * (wrap - end)
            west = pltpu.roll(end, 1, 1)
            for j in range(regs):
                centre = v[1:-1]
                if j < regs - 1:
                    following = old(j + 1, lo - 1, hi + 1)
                    flux = fe[b, j, lo:hi] * (following[1:-1] - centre)
                else:
                    following, flux = None, end
                up = fn[b, j, lo - 1 : hi] * (v[1:] - v[:-1])
                new = centre + ((flux - west) + (up[1:] - up[:-1]))
                if finish is None:
                    tmp[t % 2, j, lo:hi] = new
                else:
                    finish(j, lo, new)
                v, west = following, flux

    def step(lay, e, b):
        par = lax.rem(e, 2)
        odd = par == 1
        f, wide, span, groups = lay.f, lay.wide, lay.span, lay.groups
        own_cols = slice(EDGE, EDGE + wide)
        for d in range(8):
            only(there[-ways[d][1]], lambda d=d: halo(lay, par, b, d).wait_recv())
        f[b, 0:PASSES, own_cols] = lay.hs[par, b]
        f[b, last:deep, own_cols] = lay.hn[par, b]
        for r in range(1, deep - 1):
            a, i = (r - 1) // groups, (r - 1) % groups
            west = pltpu.roll(f[b, r, wide : wide + EDGE], wide, 1)
            far = lay.pw[par, b, a]
            far = pltpu.roll(far, lanes - wide * i, 1) if i else far
            f[b, r, 0:EDGE] = jnp.where(lane < wide, far, west)
            east = pltpu.roll(f[b, r, EDGE : 2 * EDGE], lanes - wide, 1)
            far = lay.pe[par, b, a]
            move = (lanes - wide - wide * i) % lanes
            far = pltpu.roll(far, move, 1) if move else far
            f[b, r, wide + EDGE : span] = jnp.where(lane >= lanes - wide, far, east)
        for t in range(PASSES - 1):
            one_pass(lay, b, t, None)
        for d in range(8):
            only(there[ways[d][1]], lambda d=d: halo(lay, par, b, d).wait_send())

        def finish(j, lo, new):
            pick = pl.ds(j, SUB, stride=lay.regs)
            at_col = subs * lay.regs + j
            own_here = jnp.where((at_col >= EDGE) & (at_col < EDGE + wide), 1.0, 0.0)
            sums = None
            for i in range(new.shape[0]):
                r = lo + i
                weight = jnp.where(odd, lay.gain[b, r - PASSES, pick, :], own_here)
                weighed = new[i] * weight
                square = new[i] * weighed
                sums = square if sums is None else sums + square
                f[b, r, pick, :] = weighed
            mom[e] = mom[e] + sums

        one_pass(lay, b, PASSES - 1, finish)

        @pl.when(e < STAGES - 1)
        def _():
            emit(lay, 1 - par, b)

        @pl.when(jnp.logical_not(odd))
        def _():
            lane_all = iota((wide, lanes), 1)
            for a in range(lay.packs):
                first = PASSES + groups * a
                square = f[b, first : first + groups, own_cols].reshape(lanes, lanes).T
                pieces = [square[wide * g : wide * g + wide] for g in range(groups)]
                half = groups // 2
                while half:
                    move = half * wide
                    low = lane_all // move % 2 == 0
                    for g in range(groups):
                        if g // half % 2 == 0:
                            one, two = pieces[g], pieces[g + half]
                            pieces[g] = jnp.where(low, one, pltpu.roll(two, move, 1))
                            pieces[g + half] = jnp.where(
                                low, pltpu.roll(one, lanes - move, 1), two
                            )
                    half //= 2
                for i in range(groups):
                    begin = (lay.first + b * wide) * rows + groups * a + i
                    v_out[lax.div(e, 2), pl.ds(begin, wide, stride=rows), :] = pieces[i]

    def send_sum(k, carry):
        sum_copy(k).start()
        return carry

    def stage(e, carry):
        for lay in layouts:

            def block(b, carry, lay=lay):
                step(lay, e, b)
                return carry

            lax.fori_loop(0, lay.blocks, block, 0)
        @pl.when(e == STAGES - 2)
        def _():
            for i in range(4):
                red[i : i + 1, :] = jnp.sum(mom[i], 0, keepdims=True)
            lax.fori_loop(1, everyone, send_sum, 0)

        return carry

    lax.fori_loop(0, STAGES, stage, 0)

    total_copy = remote(red_all, red_all, sum_send, sum_recv, at(1, 0))
    total_copy.wait_recv()
    total_copy.wait_send()
    sums = jnp.sum(red[...] + jnp.sum(red_all[...], 0), 1, keepdims=True)
    m0 = sums[0:1]
    x, y, z = sums[1:2] / m0, sums[2:3] / m0, sums[3:4] / m0
    alpha = 1.0 / (1.0 + x)
    beta = (y - x * x) * alpha * alpha
    c0, c1 = 1.0 - alpha + beta, -alpha
    curve = c0 * c0 * (1.0 + x) + 2.0 * c0 * c1 * (x + y) + c1 * c1 * (y + z)
    second = beta / curve
    values = (
        alpha + second * c0,
        second * c1,
        (1.0 - second) * (1.0 - alpha) - second * beta,
        -(1.0 - second) * alpha - second * c0,
        alpha * second,
    )
    for i, value in enumerate(values):
        c_out[i : i + 1, :] = jnp.broadcast_to(value, (1, lanes))


def combine_kernel(block, v, c, increment, residual, held, sems):
    size, lanes = increment.shape
    copies = []
    for n, first in enumerate(range(0, size, block)):
        count = min(block, size - first)
        part = pl.ds(first, count)
        zero, one, two = v[0, part], v[1, part], v[2, part]
        held[0, part] = c[0:1] * zero + c[1:2] * one
        held[1, part] = c[2:3] * zero + c[3:4] * one + c[4:5] * two
        for i, target in enumerate((increment, residual)):
            copy = pltpu.make_async_copy(held.at[i, part], target.at[part], sems.at[i, n])
            copy.start()
            copies.append(copy)
    for copy in copies:
        copy.wait()


def local(
    kappa_east, kappa_north, depth, sigma, obs_precision, obs_tile, obs_col, obs_lat, innovation
):
    rows, lanes = kappa_east.shape
    total = sigma.shape[0]
    tiles, bands = lax.axis_size("lon"), lax.axis_size("lat")
    listed = obs_col.shape[0]
    cap = 2 * listed // tiles
    layouts = layouts_of(total, rows, lanes)
    channels = layouts[-1].first + layouts[-1].blocks * layouts[-1].wide
    width = -(-(-(-total // SUB) * SUB + SUB) // 128) * 128

    deep = rows + 2 * PASSES
    vmem = pl.BlockSpec(memory_space=pltpu.VMEM)
    f32 = jnp.float32
    dma = pltpu.SemaphoreType.DMA
    slots = tiles * cap
    v, c = pl.pallas_call(
        functools.partial(main_kernel, tiles, bands, cap, total),
        out_shape=[
            jax.ShapeDtypeStruct((3, channels * rows, lanes), f32),
            jax.ShapeDtypeStruct((SUB, lanes), f32),
        ],
        in_specs=[pl.BlockSpec(memory_space=pltpu.HBM)] * 9,
        out_specs=[vmem] * 2,
        scratch_shapes=[
            pltpu.VMEM((rows, lanes), jnp.int32),
            pltpu.VMEM((1, total), f32),
            pltpu.VMEM((1, total), f32),
            pltpu.VMEM((3, 1, listed), jnp.int32),
            pltpu.VMEM((total, listed), f32),
            pltpu.VMEM((3, rows, lanes), f32),
            pltpu.VMEM((width, listed), f32),
            pltpu.VMEM((SUB, -(-channels // lanes) * lanes), f32),
            pltpu.VMEM((tiles, cap + SUB, lanes), f32),
            pltpu.VMEM((tiles, cap + SUB, lanes), f32),
            pltpu.VMEM((9, 3, rows, lanes), f32),
            pltpu.VMEM((3, 3, -(-(deep + 1) // SUB) * SUB, lanes), f32),
            pltpu.VMEM((STAGES, SUB, lanes), f32),
            pltpu.VMEM((SUB, lanes), f32),
            pltpu.VMEM((tiles * bands - 1, SUB, lanes), f32),
            dma((tiles - 1,)),
            dma((tiles - 1,)),
            dma((8,)),
            dma((8,)),
            dma,
            dma((9,)),
            dma,
            dma,
        ]
        + [shape for lay in layouts for shape in lay.shapes(slots)],
        compiler_params=pltpu.CompilerParams(
            collective_id=1, has_side_effects=True, vmem_limit_bytes=48 * 1024 * 1024
        ),
        name="smooth_all",
    )(
        *[
            pltpu.with_memory_space_constraint(x, pltpu.HBM)
            for x in (
                kappa_east,
                kappa_north,
                depth,
                sigma.reshape(1, total),
                obs_precision.reshape(1, total),
                obs_tile.reshape(1, listed),
                obs_col.reshape(1, listed),
                obs_lat.reshape(1, listed),
                innovation,
            )
        ]
    )

    block = 4 * SUB * rows
    pieces = -(-total * rows // block)
    increment, residual = pl.pallas_call(
        functools.partial(combine_kernel, block),
        out_shape=[jax.ShapeDtypeStruct((total * rows, lanes), f32)] * 2,
        in_specs=[vmem] * 2,
        out_specs=[pl.BlockSpec(memory_space=pl.ANY)] * 2,
        scratch_shapes=[pltpu.VMEM((2, total * rows, lanes), f32), dma((2, pieces))],
        compiler_params=pltpu.CompilerParams(vmem_limit_bytes=10 * 1024 * 1024),
        name="combine",
    )(v, c)
    shape = (total, rows, lanes)
    return increment.reshape(shape), residual.reshape(shape)


def solution(mesh):
    return jax.shard_map(
        local,
        mesh=mesh,
        in_specs=(
            P("lat", "lon"),
            P("lat", "lon"),
            P("lat", "lon"),
            P(),
            P(),
            P(("lon", "lat"), None),
            P(("lon", "lat")),
            P(("lon", "lat")),
            P(None, ("lon", "lat")),
        ),
        out_specs=(P(None, "lat", "lon"), P(None, "lat", "lon")),
        check_vma=False,
    )
```

time: 60.2 us -> 56.5 us (0.939)
  Pallas kernels: 59.4 us -> 55.7 us
    pallas_call x1, Pallas kernels: 57.8 us -> 54.1 us  [local(): pl.pallas_call(functools.partial(main_kernel, tiles, bands, cap, total),...]
where the time goes in v3:
time: 56.5 us; the launch traced here: 56.3 us
  Pallas kernels  55.7 us (99%)
  between operations  0.64 us (1%)
    pallas_call x1, Pallas kernels, local(): pl.pallas_call(functools.partial(main_kernel, tiles, bands, cap, total),...  54.1 us
    pallas_call x1, Pallas kernels, local(): pl.pallas_call(functools.partial(combine_kernel, block), out_shape=[jax.S...  1.6 us

profile of v3, /device:TPU:0, one launch (start us, length us, event | category | flops | bytes accessed | tf_op | source)
XLA Modules:
  0.0 56.3 jit_solution(10821043841806188735)
XLA Ops:
  0.6 54.1 %smooth_all.1 = (f32[3,2560,128]{2,1,0:T(8,128)S(1)}, f32[8,128]{1,0:T(8,128)S(1)}) custom-call(f32[16,128]{1,0:T(8,128)} %ke_in.1, f32[16,128]{1,0:T(8,128)} %kn_in.1, s32[16,128]{1,0:T(8,128)} %depth_in.1, f32[1,151]{1,0:T(1,128)} %bitcast.7, f32[1,151]{1,0:T(1,128)} %bitcast.8, s32[1,128]{1,0:T(1,128)} %bitcast.9, s32[1,128]{1,0:T(1,128)} %bitcast.10, ...), custom_call_target="tpu_custom_call" | custom-call | tf_op jit(solution)/shard_map/smooth_all/pallas_call | solution.py:667
  54.7 1.6 %combine.1 = (f32[2416,128]{1,0:T(8,128)}, f32[2416,128]{1,0:T(8,128)}) custom-call(f32[3,2560,128]{2,1,0:T(8,128)S(1)} %get-tuple-element.6.v, f32[8,128]{1,0:T(8,128)S(1)} %get-tuple-element.7.c), custom_call_target="tpu_custom_call" | custom-call | tf_op jit(solution)/shard_map/combine/pallas_call | solution.py:724

commit v4 on v3

--- a/solution.py
+++ b/solution.py
@@ -14,7 +14,7 @@
 EDGE = 8
 
 
-SCRATCH = ("base", "values", "coef", "f", "fe", "fn", "tmp", "gain")
+SCRATCH = ("base", "values", "cell", "coef", "f", "fe", "fn", "tmp", "gain")
 SCRATCH += ("hs", "hn", "pw", "pe", "pk", "send", "recv")
 
 
@@ -42,6 +42,7 @@
         return [
             pltpu.VMEM((5, deep, self.span, lanes), f32),
             pltpu.VMEM((3, slots, (blocks + 1) * lanes), jnp.bfloat16),
+            pltpu.VMEM((rows * self.wide, slots), jnp.bfloat16),
             pltpu.VMEM((blocks, SUB, lanes), f32),
             pltpu.VMEM((blocks, deep, self.span, lanes), f32),
             faces,
@@ -119,6 +120,7 @@
     ext,
     mom,
     red,
+    red_pair,
     red_all,
     obs_send,
     obs_recv,
@@ -176,12 +178,22 @@
     def greet(peer):
         pl.semaphore_signal(barrier, inc=1, device_id=peer, device_id_type=MESH)
 
-    def greet_all(k, carry):
-        peer = lax.rem(lon * bands + lat + k, tiles * bands)
-        greet((lax.div(peer, bands), lax.rem(peer, bands)))
+    half = bands // 2
+    kin = tiles * half
+    me = lon * half + lax.div(lat, 2)
+
+    def kin_of(k):
+        peer = lax.rem(me + k, kin)
+        return lax.div(peer, half), 2 * lax.rem(peer, half) + lax.rem(lat, 2)
+
+    def greet_kin(k, carry):
+        greet(kin_of(k))
         return carry
 
-    lax.fori_loop(1, tiles * bands, greet_all, 0)
+    lax.fori_loop(1, kin, greet_kin, 0)
+    for dl, db in ways:
+        if db:
+            only(there[db], functools.partial(greet, at(dl, db)))
 
     def remote(src, dst, send, recv, peer):
         return pltpu.make_async_remote_copy(
@@ -237,7 +249,8 @@
             piece = pltpu.roll(packed[n, SUB * i : SUB * i + SUB, lanes:], share * i, 1)
             out = jnp.where(low >= share * i, piece, out)
         pay[n, cap:] = out
-    pl.semaphore_wait(barrier, tiles * bands - 1)
+    greeted = jnp.where(has_s, 3, 0) + jnp.where(has_n, 3, 0)
+    pl.semaphore_wait(barrier, kin - 1 + greeted)
     obs = []
     for k, peer in enumerate(along):
         copy = remote(pay.at[peer[0]], rcv.at[lon], obs_send.at[k], obs_recv.at[k], peer)
@@ -320,9 +333,30 @@
             piece = out[:, lanes * i : lanes * i + lanes].reshape(rows, SUB, lanes)
             lay.base[4, PASSES:last, EDGE + SUB * i : EDGE + SUB * i + SUB] = piece
 
+    for lay in layouts:
+        flat = (lay.blocks + 1) * lanes
+        source, goal = iota((width, flat), 0), iota((width, flat), 1)
+        channel = goal // lanes * lay.wide + goal % lay.wide + lay.first
+        channel = jnp.where(goal < lay.blocks * lanes, channel, kinds_at)
+        lay.to_flat = ones_where(source == channel)
+
     own.wait()
     for copy in obs:
         copy.wait()
+    def cells_of(lay, first, end, count):
+        out = None
+        for i in range(count):
+            part = jnp.dot(
+                lay.cell[...],
+                lay.values[i, :, first * lanes : end * lanes],
+                preferred_element_type=jnp.float32,
+            )
+            out = part if i == 0 else out + part
+        return [
+            out[:, n * lanes : (n + 1) * lanes].reshape(rows, lay.wide, lanes)
+            for n in range(end - first)
+        ]
+
     first_half = rcv[:, 0:cap].reshape(slots, lanes)
     second = []
     for n in range(tiles):
@@ -343,36 +377,20 @@
     for lay in layouts:
         wide, blocks = lay.wide, lay.blocks
         flat = (blocks + 1) * lanes
-        source, goal = iota((width, flat), 0), iota((width, flat), 1)
-        channel = goal // lanes * wide + goal % wide + lay.first
-        to_flat = ones_where(source == jnp.where(goal < blocks * lanes, channel, kinds_at))
         group = (iota((slots, flat), 1) % lanes // wide * wide).astype(jnp.float32)
         mine = (columns >= group) & (columns < group + wide)
         for i, piece in enumerate(pieces):
-            wide_part = jnp.dot(piece, to_flat, preferred_element_type=jnp.float32)
+            wide_part = jnp.dot(piece, lay.to_flat, preferred_element_type=jnp.float32)
             lay.values[i] = jnp.where(mine, wide_part, 0.0).astype(jnp.bfloat16)
         place = turned[1:2] * wide + turned[0:1] - jnp.floor(turned[0:1] / wide) * wide
         spots = iota((rows * wide, slots), 0).astype(jnp.float32)
-        to_cell = ones_where(spots == place)
+        lay.cell[...] = ones_where(spots == place)
         own_cols = slice(EDGE, EDGE + wide)
         depths = lay.base[4, PASSES:last, own_cols]
-
-        def cells_of(b, count):
-            out = jnp.zeros((rows * wide, lanes), jnp.float32)
-            for i in range(count):
-                out = out + jnp.dot(
-                    to_cell,
-                    lay.values[i, :, b * lanes : (b + 1) * lanes],
-                    preferred_element_type=jnp.float32,
-                )
-            return out.reshape(rows, wide, lanes)
-
-        counts = cells_of(blocks, 1)
-        for b in range(blocks):
+        for b, cells in enumerate(cells_of(lay, 0, blocks, 3)):
             wet = depths > lay.coef[b, 0:1][None]
-            cells = lay.coef[b, 1:2][None] * cells_of(b, 3)
+            cells = lay.coef[b, 1:2][None] * cells
             lay.f[b, PASSES:last, own_cols] = jnp.where(wet, cells, 0.0)
-            lay.gain[b, :, own_cols] = jnp.where(wet, lay.coef[b, 2:3][None] * counts, 0.0)
 
     lane = iota((SUB, lanes), 1)
     subs = iota((SUB, lanes), 0)
@@ -412,6 +430,14 @@
     for lay in layouts:
         for b in range(lay.blocks):
             emit(lay, 0, b)
+
+    for lay in layouts:
+        own_cols = slice(EDGE, EDGE + lay.wide)
+        depths = lay.base[4, PASSES:last, own_cols]
+        counts = cells_of(lay, lay.blocks, lay.blocks + 1, 1)[0]
+        for b in range(lay.blocks):
+            wet = depths > lay.coef[b, 0:1][None]
+            lay.gain[b, :, own_cols] = jnp.where(wet, lay.coef[b, 2:3][None] * counts, 0.0)
 
     for d in range(8):
         dl, db = ways[d]
@@ -478,14 +504,12 @@
     for lay in layouts:
         lax.fori_loop(0, lay.blocks, functools.partial(build, lay), 0)
 
-    everyone = tiles * bands
-    me = lon * bands + lat
+    def pair_copy():
+        partner = lat + 1 - 2 * lax.rem(lat, 2)
+        return remote(red, red_pair, sum_send.at[0], sum_recv.at[0], (lon, partner))
 
     def sum_copy(k):
-        peer = lax.rem(me + k, everyone)
-        return remote(
-            red, red_all.at[k - 1], sum_send, sum_recv, (lax.div(peer, bands), lax.rem(peer, bands))
-        )
+        return remote(red, red_all.at[k - 1], sum_send.at[1], sum_recv.at[1], kin_of(k))
 
     def one_pass(lay, b, t, finish):
         f, fe, fn, tmp, regs = lay.f, lay.fe, lay.fn, lay.tmp, lay.regs
@@ -595,6 +619,14 @@
 
             def block(b, carry, lay=lay):
                 step(lay, e, b)
+                if lay is layouts[0]:
+
+                    @pl.when((e == STAGES - 1) & (b == 0))
+                    def _():
+                        pair_copy().wait()
+                        red[...] = red[...] + red_pair[...]
+                        lax.fori_loop(1, kin, send_sum, 0)
+
                 return carry
 
             lax.fori_loop(0, lay.blocks, block, 0)
@@ -602,13 +634,13 @@
         def _():
             for i in range(4):
                 red[i : i + 1, :] = jnp.sum(mom[i], 0, keepdims=True)
-            lax.fori_loop(1, everyone, send_sum, 0)
+            pair_copy().start()
 
         return carry
 
     lax.fori_loop(0, STAGES, stage, 0)
 
-    total_copy = remote(red_all, red_all, sum_send, sum_recv, at(1, 0))
+    total_copy = remote(red_all, red_all, sum_send.at[1], sum_recv.at[1], at(1, 0))
     total_copy.wait_recv()
     total_copy.wait_send()
     sums = jnp.sum(red[...] + jnp.sum(red_all[...], 0), 1, keepdims=True)
@@ -687,15 +719,16 @@
             pltpu.VMEM((3, 3, -(-(deep + 1) // SUB) * SUB, lanes), f32),
             pltpu.VMEM((STAGES, SUB, lanes), f32),
             pltpu.VMEM((SUB, lanes), f32),
-            pltpu.VMEM((tiles * bands - 1, SUB, lanes), f32),
+            pltpu.VMEM((SUB, lanes), f32),
+            pltpu.VMEM((tiles * bands // 2 - 1, SUB, lanes), f32),
             dma((tiles - 1,)),
             dma((tiles - 1,)),
             dma((8,)),
             dma((8,)),
             dma,
             dma((9,)),
-            dma,
-            dma,
+            dma((2,)),
+            dma((2,)),
         ]
         + [shape for lay in layouts for shape in lay.shapes(slots)],
         compiler_params=pltpu.CompilerParams(

time: 56.5 us -> 55.1 us (0.975)
  Pallas kernels: 55.7 us -> 54.2 us
    pallas_call x1, Pallas kernels: 54.1 us -> 52.6 us  [local(): pl.pallas_call(functools.partial(main_kernel, tiles, bands, cap, total),...]
where the time goes in v4:
time: 55.1 us; the launch traced here: 54.9 us
  Pallas kernels  54.2 us (98%)
  between operations  0.64 us (1%)
    pallas_call x1, Pallas kernels, local(): pl.pallas_call(functools.partial(main_kernel, tiles, bands, cap, total),...  52.6 us
    pallas_call x1, Pallas kernels, local(): pl.pallas_call(functools.partial(combine_kernel, block), out_shape=[jax.S...  1.6 us

profile of v4, /device:TPU:0, one launch (start us, length us, event | category | flops | bytes accessed | tf_op | source)
XLA Modules:
  0.0 54.9 jit_solution(3630350937709113675)
XLA Ops:
  0.6 52.6 %smooth_all.1 = (f32[3,2560,128]{2,1,0:T(8,128)S(1)}, f32[8,128]{1,0:T(8,128)S(1)}) custom-call(f32[16,128]{1,0:T(8,128)} %ke_in.1, f32[16,128]{1,0:T(8,128)} %kn_in.1, s32[16,128]{1,0:T(8,128)} %depth_in.1, f32[1,151]{1,0:T(1,128)} %bitcast.7, f32[1,151]{1,0:T(1,128)} %bitcast.8, s32[1,128]{1,0:T(1,128)} %bitcast.9, s32[1,128]{1,0:T(1,128)} %bitcast.10, ...), custom_call_target="tpu_custom_call" | custom-call | tf_op jit(solution)/shard_map/smooth_all/pallas_call | solution.py:699
  53.3 1.6 %combine.1 = (f32[2416,128]{1,0:T(8,128)}, f32[2416,128]{1,0:T(8,128)}) custom-call(f32[3,2560,128]{2,1,0:T(8,128)S(1)} %get-tuple-element.6.v, f32[8,128]{1,0:T(8,128)S(1)} %get-tuple-element.7.c), custom_call_target="tpu_custom_call" | custom-call | tf_op jit(solution)/shard_map/combine/pallas_call | solution.py:757

commit v5 on v4

--- a/solution.py
+++ b/solution.py
@@ -76,7 +76,7 @@
     return high, middle, low
 
 
-def chunks(first, end, most=8):
+def chunks(first, end, most=5):
     count = -(-(end - first) // most)
     cuts = [first + (end - first) * i // count for i in range(count + 1)]
     return list(zip(cuts[:-1], cuts[1:]))
@@ -144,7 +144,7 @@
     def at(dl, db):
         return lax.rem(lon + dl + tiles, tiles), lax.rem(lat + db + bands, bands)
 
-    along = [(lax.rem(lon + k, tiles), lat) for k in range(1, tiles)]
+    along = [(lax.rem(lon + k, tiles), lat) for k in sorted(range(1, tiles), key=lambda k: abs(2 * k - tiles))]
     ways = [(0, -1), (0, 1), (-1, 0), (1, 0), (-1, -1), (1, -1), (-1, 1), (1, 1)]
     there = {-1: has_s, 0: None, 1: has_n}
 

time: 55.1 us -> 54.9 us (level)
  no operation moved by 1% of the time
where the time goes in v5:
time: 54.9 us; the launch traced here: 54.7 us
  Pallas kernels  54 us (98%)
  between operations  0.64 us (1%)
    pallas_call x1, Pallas kernels, local(): pl.pallas_call(functools.partial(main_kernel, tiles, bands, cap, total),...  52.4 us
    pallas_call x1, Pallas kernels, local(): pl.pallas_call(functools.partial(combine_kernel, block), out_shape=[jax.S...  1.6 us

profile of v5, /device:TPU:0, one launch (start us, length us, event | category | flops | bytes accessed | tf_op | source)
XLA Modules:
  0.0 54.7 jit_solution(5379160971694596930)
XLA Ops:
  0.6 52.4 %smooth_all.1 = (f32[3,2560,128]{2,1,0:T(8,128)S(1)}, f32[8,128]{1,0:T(8,128)S(1)}) custom-call(f32[16,128]{1,0:T(8,128)} %ke_in.1, f32[16,128]{1,0:T(8,128)} %kn_in.1, s32[16,128]{1,0:T(8,128)} %depth_in.1, f32[1,151]{1,0:T(1,128)} %bitcast.7, f32[1,151]{1,0:T(1,128)} %bitcast.8, s32[1,128]{1,0:T(1,128)} %bitcast.9, s32[1,128]{1,0:T(1,128)} %bitcast.10, ...), custom_call_target="tpu_custom_call" | custom-call | tf_op jit(solution)/shard_map/smooth_all/pallas_call | solution.py:699
  53.1 1.6 %combine.1 = (f32[2416,128]{1,0:T(8,128)}, f32[2416,128]{1,0:T(8,128)}) custom-call(f32[3,2560,128]{2,1,0:T(8,128)S(1)} %get-tuple-element.6.v, f32[8,128]{1,0:T(8,128)S(1)} %get-tuple-element.7.c), custom_call_target="tpu_custom_call" | custom-call | tf_op jit(solution)/shard_map/combine/pallas_call | solution.py:757

commit v6 on v5

--- a/solution.py
+++ b/solution.py
@@ -547,17 +547,22 @@
         odd = par == 1
         f, wide, span, groups = lay.f, lay.wide, lay.span, lay.groups
         own_cols = slice(EDGE, EDGE + wide)
-        for d in range(8):
+        for d in (0, 1):
             only(there[-ways[d][1]], lambda d=d: halo(lay, par, b, d).wait_recv())
         f[b, 0:PASSES, own_cols] = lay.hs[par, b]
         f[b, last:deep, own_cols] = lay.hn[par, b]
         for r in range(1, deep - 1):
+            f[b, r, 0:EDGE] = pltpu.roll(f[b, r, wide : wide + EDGE], wide, 1)
+            f[b, r, wide + EDGE : span] = pltpu.roll(f[b, r, EDGE : 2 * EDGE], lanes - wide, 1)
+        for d in range(2, 8):
+            only(there[-ways[d][1]], lambda d=d: halo(lay, par, b, d).wait_recv())
+        for r in range(1, deep - 1):
             a, i = (r - 1) // groups, (r - 1) % groups
-            west = pltpu.roll(f[b, r, wide : wide + EDGE], wide, 1)
+            west = f[b, r, 0:EDGE]
             far = lay.pw[par, b, a]
             far = pltpu.roll(far, lanes - wide * i, 1) if i else far
             f[b, r, 0:EDGE] = jnp.where(lane < wide, far, west)
-            east = pltpu.roll(f[b, r, EDGE : 2 * EDGE], lanes - wide, 1)
+            east = f[b, r, wide + EDGE : span]
             far = lay.pe[par, b, a]
             move = (lanes - wide - wide * i) % lanes
             far = pltpu.roll(far, move, 1) if move else far
@@ -752,7 +757,7 @@
         ]
     )
 
-    block = 4 * SUB * rows
+    block = 2 * SUB * rows
     pieces = -(-total * rows // block)
     increment, residual = pl.pallas_call(
         functools.partial(combine_kernel, block),

time: 54.9 us -> 54.7 us (level)
  no operation moved by 1% of the time
where the time goes in v6:
time: 54.7 us; the launch traced here: 54.5 us
  Pallas kernels  53.8 us (98%)
  between operations  0.64 us (1%)
    pallas_call x1, Pallas kernels, local(): pl.pallas_call(functools.partial(main_kernel, tiles, bands, cap, total),...  52.2 us
    pallas_call x1, Pallas kernels, local(): pl.pallas_call(functools.partial(combine_kernel, block), out_shape=[jax.S...  1.63 us

profile of v6, /device:TPU:0, one launch (start us, length us, event | category | flops | bytes accessed | tf_op | source)
XLA Modules:
  0.0 54.5 jit_solution(13334434833638009319)
XLA Ops:
  0.6 52.2 %smooth_all.1 = (f32[3,2560,128]{2,1,0:T(8,128)S(1)}, f32[8,128]{1,0:T(8,128)S(1)}) custom-call(f32[16,128]{1,0:T(8,128)} %ke_in.1, f32[16,128]{1,0:T(8,128)} %kn_in.1, s32[16,128]{1,0:T(8,128)} %depth_in.1, f32[1,151]{1,0:T(1,128)} %bitcast.7, f32[1,151]{1,0:T(1,128)} %bitcast.8, s32[1,128]{1,0:T(1,128)} %bitcast.9, s32[1,128]{1,0:T(1,128)} %bitcast.10, ...), custom_call_target="tpu_custom_call" | custom-call | tf_op jit(solution)/shard_map/smooth_all/pallas_call | solution.py:704
  52.8 1.6 %combine.1 = (f32[2416,128]{1,0:T(8,128)}, f32[2416,128]{1,0:T(8,128)}) custom-call(f32[3,2560,128]{2,1,0:T(8,128)S(1)} %get-tuple-element.6.v, f32[8,128]{1,0:T(8,128)S(1)} %get-tuple-element.7.c), custom_call_target="tpu_custom_call" | custom-call | tf_op jit(solution)/shard_map/combine/pallas_call | solution.py:762
